TPU v7x, 128 devices: a whole 4x4x4 slice. The times are simulated.
128 devices in a mesh: tile: 16 (over y, z), layer: 8 (over x, core).
Axes of the slice: x: 4, y: 4, z: 4, core: 2. Of those that a mesh axis runs over, the one named last changes fastest.
Arguments:
- velocity_guess: float32 [2, 128, 3072], P(None, 'tile'), may hold values from -6 to 6
- hardness: float32 [32, 128, 3072], P('layer', 'tile'), may hold values from 0.7 to 1.5
- thickness: float32 [128, 3072], P('tile'), may hold values from 0.5 to 2
- friction: float32 [128, 3072], P('tile'), may hold values from 0.5 to 5
- grounded: int32 [128, 3072], P('tile'), may hold values 0 or 1
- ice_mask: int32 [128, 3072], P('tile'), may hold values 0 or 1
- driving: float32 [2, 128, 3072], P(None, 'tile'), may hold values from -8 to 8
- obs_cell: int32 [16, 8, 16, 512], P('tile', 'layer'), may hold values from 0 to 24575
- obs_east: float32 [16, 8, 16, 512], P('tile', 'layer'), may hold values from -6 to 6
- obs_north: float32 [16, 8, 16, 512], P('tile', 'layer'), may hold values from -6 to 6
- obs_weight: float32 [16, 8, 16, 512], P('tile', 'layer'), may hold values from 0.1 to 1
- obs_count: int32 [16, 8, 16], P('tile', 'layer'), may hold values from 64 to 512, as said below
Outputs:
- velocity: float32 [2, 128, 3072], P(None, 'tile')
- friction_gradient: float32 [128, 3072], P('tile')
Inputs may be any that keep to these rules, and one draw needn't show every extreme that they name: `obs_count`: counts lie between 64 and 512; in every draw one destination strip receives full blocks from every device. `obs_cell`: cells are numbered row by row within the destination strip.
All inputs are finite; a program needn't handle non-finite values. No bound on the sum of `grounded` or of `ice_mask` on one device may be relied on, other than what follows from the above.
Results may differ from a plain program's by a relative error of at most 0.00013.
Values sent between devices are 32-bit elements; how exact they have to be, the bound alone decides.
No kernel may reach another device: no remote copies, remote signals or barrier semaphores. Data moves between devices by JAX's collectives and lax.ppermute only.
A program may use at most 64 MiB of HBM per device.

v0:
```python
import jax
import jax.numpy as jnp
from jax import lax
from jax.sharding import PartitionSpec as P

SWEEPS = 40


OMEGA = 0.5
REGULAR = 0.01


def padded(array, sides, width):
    for axis, dim in sides:
        count, length = (lax.axis_size(axis), array.shape[dim])
        up = [(i, (i + 1) % count) for i in range(count - 1)]
        down = [(j, i) for i, j in up]
        last = lax.slice_in_dim(array, length - width, length, axis=dim)
        leading = lax.slice_in_dim(array, 0, width, axis=dim)
        before = lax.ppermute(last, axis, up)
        after = lax.ppermute(leading, axis, down)
        array = jnp.concatenate([before, array, after], axis=dim)
    return array


def pad_cols(field):
    return jnp.pad(field, ((0, 0), (1, 1)))


def col_diff(field):
    wide = pad_cols(field)
    return 0.5 * (wide[:, 2:] - wide[:, :-2])


def row_diff(field):
    return 0.5 * (field[2:] - field[:-2])


def strain_rate(east_vel, north_vel):
    slope_ux = row_diff(east_vel)
    slope_vx = row_diff(north_vel)
    slope_uy = col_diff(east_vel[1:-1])
    slope_vy = col_diff(north_vel[1:-1])
    shear = slope_uy + slope_vx
    return (
        slope_ux * slope_ux
        + slope_vy * slope_vy
        + slope_ux * slope_vy
        + 0.25 * shear * shear
        + REGULAR
    )


def sweep(east_vel, north_vel, viscous, force_east, force_north, drag, inside):
    centre_visc = viscous[1:-1]
    wide_visc = pad_cols(centre_visc)
    face_north = 0.5 * (centre_visc + viscous[2:])
    face_south = 0.5 * (centre_visc + viscous[:-2])
    face_east = 0.5 * (centre_visc + wide_visc[:, 2:])
    face_west = 0.5 * (centre_visc + wide_visc[:, :-2])
    drag_mid = drag[1:-1]
    inside_mid = inside[1:-1]

    def laplace(field, row_gain, col_gain):
        centre = field[1:-1]
        wide = pad_cols(centre)
        rows_part = face_north * (centre - field[2:]) + face_south * (centre - field[:-2])
        cols_part = face_east * (centre - wide[:, 2:]) + face_west * (centre - wide[:, :-2])
        return row_gain * rows_part + col_gain * cols_part + drag_mid * centre

    cross_east = row_diff(2.0 * viscous * col_diff(north_vel)) + col_diff(
        centre_visc * row_diff(north_vel)
    )
    cross_north = col_diff(2.0 * centre_visc * row_diff(east_vel)) + row_diff(
        viscous * col_diff(east_vel)
    )
    resid_east = force_east[1:-1] - (laplace(east_vel, 4.0, 1.0) - cross_east)
    resid_north = force_north[1:-1] - (laplace(north_vel, 1.0, 4.0) - cross_north)
    diag_east = (
        4.0 * (face_north + face_south) + face_east + face_west + drag_mid + 1.0 - inside_mid
    )
    diag_north = (
        face_north + face_south + 4.0 * (face_east + face_west) + drag_mid + 1.0 - inside_mid
    )
    new_east = inside_mid * (east_vel[1:-1] + OMEGA * resid_east / diag_east)
    new_north = inside_mid * (north_vel[1:-1] + OMEGA * resid_north / diag_north)
    return jnp.stack([new_east, new_north], 0)


def relax(start, forces, viscous, drag, inside):

    def outer_single(step, fields):
        wide = padded(fields, (("tile", 1),), 1)
        return sweep(wide[0], wide[1], viscous, forces[0], forces[1], drag, inside)

    return lax.fori_loop(0, SWEEPS, outer_single, start)


def on_device(
    velocity_guess,
    hardness,
    thickness,
    friction,
    grounded,
    ice_mask,
    driving,
    obs_cell,
    obs_east,
    obs_north,
    obs_weight,
    obs_count,
):
    depth = 1
    rows_here = thickness.shape[0]
    cols_here = thickness.shape[1]
    drag = friction * grounded.astype(jnp.float32)
    inside = ice_mask.astype(jnp.float32)
    stacked = jnp.concatenate(
        [velocity_guess, thickness[None], drag[None], inside[None], driving, hardness], 0
    )
    extended = padded(stacked, (("tile", 1),), depth + 1)
    valid = (lax.broadcasted_iota(jnp.int32, obs_weight.shape, 3) < obs_count[..., None]).astype(
        jnp.float32
    )
    packed = jnp.stack([obs_cell.astype(jnp.float32), obs_east, obs_north, obs_weight * valid], 0)
    arrived = lax.all_to_all(packed, "tile", split_axis=3, concat_axis=1, tiled=True)
    rate = jnp.power(strain_rate(extended[0], extended[1]), -1.0 / 3.0)
    partial_sum = 0.5 * rate * jnp.sum(extended[7:, 1:-1], axis=0)
    layers_all = hardness.shape[0] * lax.axis_size("layer")
    cells = arrived[0].reshape(-1).astype(jnp.int32)
    weights = arrived[3].reshape(-1)
    total = lax.psum(partial_sum, "layer")
    viscous = extended[2, 1:-1] * total / layers_all
    drag_ext = extended[3, 1:-1]
    inside_ext = extended[4, 1:-1]
    forces = extended[5:7, 1:-1]
    velocity = relax(velocity_guess, forces, viscous, drag_ext, inside_ext)
    flat_east = velocity[0].reshape(-1)
    flat_north = velocity[1].reshape(-1)
    term_east = weights * (flat_east[cells] - arrived[1].reshape(-1))
    term_north = weights * (flat_north[cells] - arrived[2].reshape(-1))
    misfit_east = jax.ops.segment_sum(term_east, cells, num_segments=rows_here * cols_here)
    misfit_north = jax.ops.segment_sum(term_north, cells, num_segments=rows_here * cols_here)
    misfit_east, misfit_north = (misfit_east, misfit_north)
    summed = lax.psum((misfit_east, misfit_north), "layer")
    source = jnp.stack(
        [summed[0].reshape(rows_here, cols_here), summed[1].reshape(rows_here, cols_here)], 0
    )
    source_ext = jnp.pad(source, ((0, 0), (1, 1), (0, 0)))
    adjoint = relax(jnp.zeros_like(source), source_ext, viscous, drag_ext, inside_ext)
    drag_own = drag_ext[depth : depth + rows_here]
    gradient = -(drag_own * (velocity[0] * adjoint[0] + velocity[1] * adjoint[1]))
    return (velocity, gradient)


def solution(mesh):
    return jax.shard_map(
        on_device,
        mesh=mesh,
        in_specs=(
            P(None, "tile", None),
            P("layer", "tile", None),
            P("tile", None),
            P("tile", None),
            P("tile", None),
            P("tile", None),
            P(None, "tile", None),
            P("tile", "layer", None, None),
            P("tile", "layer", None, None),
            P("tile", "layer", None, None),
            P("tile", "layer", None, None),
            P("tile", "layer", None),
        ),
        out_specs=(P(None, "tile", None), P("tile", None)),
        check_vma=False,
    )
```

profile of v0, /device:TPU:96, one launch (start us, length us, event | category | flops | bytes accessed | tf_op | source)
XLA Modules:
  0.0 1243.4 jit_solution(12809235096810841908)
XLA Ops:
  12.2 7.2 all-to-all-start
  25.8 4.1 collective-permute-done.4
  29.8 4.7 collective-permute-done.5
  38.6 59.4 %all-reduce.21.cloned.1.call-done = f32[10,3072]{1,0:T(8,128)} async-done(((f32[10,3072]{1,0:T(8,128)}), f32[10,3072]{1,0:T(8,128)}) %all-reduce.21.cloned.1.call-update) | async-done | bytes 122896 | tf_op jit(solution)/shard_map/psum | solution.py:132
  99.0 449.2 %while.24 = (s32[]{:T(128)}, f32[2,8,3072]{2,1,0:T(8,128)S(1)}, f32[10,3072]{1,0:T(8,128)S(1)}, f32[2,10,3072]{2,1,0:T(8,128)S(1)}, f32[8,3072]{1,0:T(8,128)S(1)...) while((s32[]{:T(128)}, f32[2,8,3072]{2,1,0:T(8,128)S(1)}, ...), condition=%wide.region_3.4_spmd, body=%wide.region_2.3_spmd.sunk | while | flops 2476034 | bytes 6734017 | solution.py:96
  105.0 5.0 collective-permute-done
  113.4 3.9 collective-permute-start
  124.6 3.9 collective-permute-start
  135.8 3.9 collective-permute-start
  147.0 3.9 collective-permute-start
  158.2 3.9 collective-permute-start
  169.4 3.9 collective-permute-start
  180.6 3.9 collective-permute-start
  191.8 3.9 collective-permute-start
  202.9 3.9 collective-permute-start
  214.1 3.9 collective-permute-start
  225.3 3.9 collective-permute-start
  236.5 3.9 collective-permute-start
  247.7 3.9 collective-permute-start
  258.9 3.9 collective-permute-start
  270.1 3.9 collective-permute-start
  281.3 3.9 collective-permute-start
  292.5 3.9 collective-permute-start
  303.7 3.9 collective-permute-start
  314.9 3.9 collective-permute-start
  326.1 3.9 collective-permute-start
  337.2 3.9 collective-permute-start
  348.4 3.9 collective-permute-start
  359.6 3.9 collective-permute-start
  370.9 3.9 collective-permute-start
  382.1 3.9 collective-permute-start
  393.3 3.9 collective-permute-start
  404.5 3.9 collective-permute-start
  415.7 3.9 collective-permute-start
  426.9 3.9 collective-permute-start
  438.1 3.9 collective-permute-start
  449.2 3.9 collective-permute-start
  460.4 3.9 collective-permute-start
  464.5 4.0 collective-permute-done
  471.9 3.9 collective-permute-start
  527.8 3.9 collective-permute-start
  539.0 3.9 collective-permute-start
  548.3 45.5 %gather_fusion = f32[8192]{0:T(1024)S(1)} fusion(f32[24576]{0:T(1024)S(1)} %bitcast.191, s32[8192]{0:T(1024)S(1)} %broadcast_clamp_fusion), kind=kCustom, calls=%fused_computation | custom fusion | bytes 98304 | tf_op jit(solution)/shard_map/gather | solution.py:140
  593.9 45.5 %gather_fusion.1 = f32[8192]{0:T(1024)S(1)} fusion(f32[24576]{0:T(1024)S(1)} %bitcast.192, s32[8192]{0:T(1024)S(1)} %broadcast_clamp_fusion), kind=kCustom, calls=%fused_computation.1 | custom fusion | bytes 98304 | tf_op jit(solution)/shard_map/gather | solution.py:141
  639.4 43.2 %scatter_custom_fusion = f32[24576]{0:T(1024)S(1)} fusion(s32[8192]{0:T(1024)S(1)} %bitcast.198, f32[8192]{0:T(1024)S(1)} %get-tuple-element.250, f32[]{:T(128)} %constant.91.clone.1), kind=kCustom, calls=%fused_computation.200 | custom fusion | flops 8192 | bytes 98308 | tf_op jit(solution)/shard_map/scatter-add | solution.py:142
  683.3 43.2 %scatter_custom_fusion.1 = f32[24576]{0:T(1024)S(1)} fusion(s32[8192]{0:T(1024)S(1)} %bitcast.199, f32[8192]{0:T(1024)S(1)} %get-tuple-element.251, f32[]{:T(128)} %constant.91.clone.1), kind=kCustom, calls=%fused_computation.198 | custom fusion | flops 8192 | bytes 98308 | tf_op jit(solution)/shard_map/scatter-add | solution.py:143
  727.2 58.5 %all-reduce.23.cloned.1.call-done = (f32[1,8,3072]{2,1,0:T(8,128)}, f32[1,8,3072]{2,1,0:T(8,128)}) async-done(((f32[1,8,3072]{2,1,0:T(8,128)}, f32[1,8,3072]{2,1,0:T(8,128)}), (f32[1,8,3072]{2,1,0:T(8,128)}, f32[1,8,3072]{2,1,0:T(8,128)})) %all-reduce.23.cloned.1.call-update) | async-done | bytes 196624 | tf_op jit(solution)/shard_map/psum | solution.py:145
  786.7 449.2 %while.25 = (s32[]{:T(128)}, f32[2,8,3072]{2,1,0:T(8,128)S(1)}, f32[10,3072]{1,0:T(8,128)S(1)}, f32[2,10,3072]{2,1,0:T(8,128)S(1)}, f32[8,3072]{1,0:T(8,128)S(1)...) while((s32[]{:T(128)}, f32[2,8,3072]{2,1,0:T(8,128)S(1)}, ...), condition=%wide.region_9.10_spmd, body=%wide.region_8.9_spmd.sunk | while | flops 2476034 | bytes 6734017 | solution.py:96
  792.7 5.0 collective-permute-done.2
  801.1 3.9 collective-permute-start.2
  812.3 3.9 collective-permute-start.2
  823.5 3.9 collective-permute-start.2
  834.7 3.9 collective-permute-start.2
  1002.5 3.9 collective-permute-start.2
  1013.7 3.9 collective-permute-start.2
  1024.9 3.9 collective-permute-start.2
  1036.1 3.9 collective-permute-start.2
  1047.3 3.9 collective-permute-start.2
  1152.1 4.0 collective-permute-done.2
  1181.9 3.9 collective-permute-start.2
  1193.1 3.9 collective-permute-start.2
  1204.3 3.9 collective-permute-start.2
  1215.5 3.9 collective-permute-start.2
  1226.7 3.9 collective-permute-start.2
  (1202 shorter events, 699.2 us)
Async XLA Ops:
  12.2 13.4 %all-to-all-start = ((f32[4,1,1,16,512]{4,2,1,0,3:T(1,128)}), f32[4,1,1,16,512]{4,2,1,0,3:T(1,128)S(1)}, u32[]{:S(2)}, u32[]{:S(2)}) async-start(f32[4,1,1,16,512]{4,2,1,0,3:T(1,128)} %pad_maximum_fusion.9), calls=%async_computation | async-start | bytes 262144 | tf_op jit(solution)/shard_map/all_to_all | solution.py:126
  19.4 78.6 %all-reduce.21.cloned.1.call-start = ((), (), s32[]{:S(2)}) async-start(), calls=%async_computation.1 | async-start | bytes 393216 | tf_op jit(solution)/shard_map/psum | solution.py:132
  19.8 10.0 collective-permute-start.4
  23.2 11.4 collective-permute-start.5
  37.5 748.2 %all-reduce.23.cloned.1.call-start = ((), (), s32[]{:S(2)}) async-start(), calls=%async_computation.2 | async-start | bytes 393216 | tf_op jit(solution)/shard_map/psum | solution.py:145
  102.2 7.8 collective-permute-start
  113.4 7.8 collective-permute-start
  124.6 7.8 collective-permute-start
  135.8 7.8 collective-permute-start
  147.0 7.8 collective-permute-start
  158.2 7.8 collective-permute-start
  169.4 7.8 collective-permute-start
  180.6 7.8 collective-permute-start
  191.8 7.8 collective-permute-start
  202.9 7.8 collective-permute-start
  214.1 7.8 collective-permute-start
  225.3 7.8 collective-permute-start
  236.5 7.8 collective-permute-start
  247.7 7.8 collective-permute-start
  258.9 7.8 collective-permute-start
  270.1 7.8 collective-permute-start
  281.3 7.8 collective-permute-start
  292.5 7.8 collective-permute-start
  303.7 7.8 collective-permute-start
  314.9 7.8 collective-permute-start
  326.1 7.8 collective-permute-start
  337.2 7.8 collective-permute-start
  348.4 7.8 collective-permute-start
  359.6 7.9 collective-permute-start
  370.9 7.8 collective-permute-start
  382.1 7.8 collective-permute-start
  393.3 7.8 collective-permute-start
  404.5 7.8 collective-permute-start
  415.7 7.8 collective-permute-start
  426.9 7.8 collective-permute-start
  438.1 7.8 collective-permute-start
  449.2 7.8 collective-permute-start
  460.4 8.1 collective-permute-start
  471.9 7.8 collective-permute-start
  483.1 7.8 collective-permute-start
  494.3 7.8 collective-permute-start
  505.5 7.8 collective-permute-start
  516.6 7.8 collective-permute-start
  527.8 7.8 collective-permute-start
  539.0 7.8 collective-permute-start
  789.9 7.8 collective-permute-start.2
  801.1 7.8 collective-permute-start.2
  812.3 7.8 collective-permute-start.2
  823.5 7.8 collective-permute-start.2
  834.7 7.8 collective-permute-start.2
  845.9 7.8 collective-permute-start.2
  857.1 7.8 collective-permute-start.2
  868.2 7.8 collective-permute-start.2
  879.4 7.8 collective-permute-start.2
  890.6 7.8 collective-permute-start.2
  901.8 7.8 collective-permute-start.2
  913.0 7.8 collective-permute-start.2
  924.2 7.8 collective-permute-start.2
  935.4 7.8 collective-permute-start.2
  946.6 7.8 collective-permute-start.2
  957.8 7.8 collective-permute-start.2
  969.0 7.8 collective-permute-start.2
  1047.3 7.9 collective-permute-start.2
  1148.1 8.1 collective-permute-start.2
  (109 other events, 1396.8 us)
Sparse Core Ops, SparseCore 0:
  37.6 60.3 all-reduce.20
  727.4 58.2 all-reduce.22
where the time goes:
time: 1250 us; the launch traced here: 1240 us
  starting transfers between devices  480 us (38%)
  waiting for transfers between devices  437 us (35%)
  other arithmetic  172 us (14%)
  local copies, waits for them, and re-layouts  131 us (10%)
  between operations  14.4 us (1%)
    ppermute x81, waiting for transfers between devices, padded(): after = lax.ppermute(leading, axis, down)  315 us
    ppermute x81, starting transfers between devices, padded(): after = lax.ppermute(leading, axis, down)  314 us
    ppermute x81, starting transfers between devices, padded(): before = lax.ppermute(last, axis, up)  159 us
    psum x1, waiting for transfers between devices, on_device(): total = lax.psum(partial_sum, 'layer')  59.4 us
    psum x1, waiting for transfers between devices, on_device(): summed = lax.psum((misfit_east, misfit_north), 'layer')  58.5 us
    gather x1, local copies, waits for them, and re-layouts, on_device(): term_north = weights * (flat_north[cells] - arrived[2].reshape(-1))  45.5 us
    gather x1, local copies, waits for them, and re-layouts, on_device(): term_east = weights * (flat_east[cells] - arrived[1].reshape(-1))  45.5 us
    another operation x240, other arithmetic, sweep(): return jnp.stack([new_east, new_north], 0)  43.9 us
  transfers between devices with their start and end apart: 165, of which 86 were waited for; matrix products, arithmetic and copies ran while one was open for 0% of the time, Pallas kernels for 0%

commit v1 on v0

v1 whole, which is shorter than its diff:
```python
import jax
import jax.numpy as jnp
from jax import lax
from jax.experimental import pallas as pl
from jax.experimental.pallas import tpu as pltpu
from jax.sharding import PartitionSpec as P

SWEEPS = 40
LAYERS = 32
REGULAR = 0.01

ROWS = 8
COLS = 3072
TILES = COLS // 128
N_TILE = 16
N_LAYER = 8
BLOCK = 512
CHUNK = 24
WIDE = CHUNK + 4 * SWEEPS
NARROW = CHUNK + 2 * SWEEPS
WB = WIDE // 8
NB = NARROW // 8
SHARE = COLS // N_LAYER
F32 = jnp.float32


def lane_iota():
    return lax.broadcasted_iota(jnp.int32, (8, 128), 1)


def lanes_left(x, by):
    by = by % 128
    return pltpu.roll(x, 128 - by, 1) if by else x


def pack_obs_kernel(count_ref, cell_ref, east_ref, north_ref, weight_ref, out_ref):
    row = lax.broadcasted_iota(jnp.int32, (N_TILE, BLOCK), 0)
    slot = lax.broadcasted_iota(jnp.int32, (N_TILE, BLOCK), 1)
    count = jnp.zeros((N_TILE, BLOCK), jnp.int32)
    for d in range(N_TILE):
        count = jnp.where(row == d, count_ref[0, d], count)
    weight = jnp.where(slot < count, weight_ref[...], 0.0)
    cell = cell_ref[...]
    high = cell >> 7
    strip_row = ((cell >> 10) * 11) >> 5
    place = ((high - strip_row * TILES) * ROWS + strip_row) * 128 + (cell & 127)
    out_ref[:, 0:BLOCK] = place.astype(F32)
    out_ref[:, BLOCK : 2 * BLOCK] = weight
    out_ref[:, 2 * BLOCK : 3 * BLOCK] = weight * east_ref[...]
    out_ref[:, 3 * BLOCK : 4 * BLOCK] = weight * north_ref[...]


def layer_windows_kernel(hard_ref, out_ref):
    for g in range(TILES):
        at = slice(128 * g, 128 * g + 128)
        part = (hard_ref[0, :, at] + hard_ref[1, :, at]) + (hard_ref[2, :, at] + hard_ref[3, :, at])
        for dest in range(N_LAYER):
            k = g - (3 * dest - 1)
            if 0 <= k < 5:
                out_ref[dest, :, 128 * k : 128 * k + 128] = part
    out_ref[0, :, 0:128] = jnp.zeros((8, 128), F32)
    out_ref[N_LAYER - 1, :, 512:640] = jnp.zeros((8, 128), F32)


def scatter_kernel(obs_ref, out_ref, lhs_ref, rhs_ref, acc_ref):
    acc_ref[...] = jnp.zeros_like(acc_ref)
    step16 = lax.broadcasted_iota(jnp.int32, (16, BLOCK), 0).astype(F32).astype(jnp.bfloat16)

    def rows(x):
        return jnp.broadcast_to(x, (16, BLOCK)).astype(jnp.bfloat16)

    def body(s, carry):
        place = obs_ref[pl.ds(s, 1), 0:BLOCK].astype(jnp.int32)
        high = rows((place >> 7).astype(F32))
        low = rows((place & 127).astype(F32))
        pieces = []
        for f in range(3):
            value = obs_ref[pl.ds(s, 1), (f + 1) * BLOCK : (f + 2) * BLOCK]
            for _ in range(3):
                piece = value.astype(jnp.bfloat16).astype(F32)
                pieces.append(rows(piece))
                value = value - piece
        zero = jnp.zeros((16, BLOCK), jnp.bfloat16)
        one = jnp.ones((16, BLOCK), jnp.bfloat16)
        for b in range(TILES * ROWS // 16):
            rhs_ref[16 * b : 16 * b + 16, :] = jnp.where(high == step16 + 16.0 * b, one, zero)
        for b in range(8):
            hit = low == step16 + 16.0 * b
            for k in range(9):
                lhs_ref[k * 128 + 16 * b : k * 128 + 16 * b + 16, :] = jnp.where(hit, pieces[k], zero)
        acc_ref[...] += lax.dot_general(
            lhs_ref[...], rhs_ref[...], (((1,), (1,)), ((), ())), preferred_element_type=F32
        )
        return carry

    lax.fori_loop(0, N_TILE, body, 0)
    left = lane_iota() < 64
    zero = jnp.zeros((8, 128), F32)
    for f in range(3):
        total = acc_ref[3 * f * 128 : 3 * f * 128 + 128, :]
        total = total + acc_ref[(3 * f + 1) * 128 : (3 * f + 2) * 128, :]
        total = total + acc_ref[(3 * f + 2) * 128 : (3 * f + 3) * 128, :]
        cells = total.T
        turned = [pltpu.roll(cells[8 * g : 8 * g + 8, :], 64, 1) for g in range(TILES)]
        for dest in range(N_LAYER):
            for k in range(4):
                g = 3 * dest - 1 + k
                a = turned[g] if 0 <= g < TILES else zero
                b = turned[g + 1] if g + 1 < TILES else zero
                out_ref[dest, f, :, 128 * k : 128 * k + 128] = jnp.where(left, a, b)


def map_chunks_kernel(me_ref, part_ref, guess_ref, thick_ref, fric_ref, ground_ref, ice_ref, drive_ref, out_ref):
    first = 3 * me_ref[0] - 1
    lane = lane_iota()
    fields = [[] for _ in range(7)]
    for k in range(5):
        g = first + k
        ok = jnp.logical_and(g >= 0, g < TILES)
        keep = jnp.where(ok, 1.0, 0.0).astype(F32)
        start = pl.multiple_of(jnp.clip(g, 0, TILES - 1) * 128, 128)
        at = pl.ds(start, 128)
        total = part_ref[0, :, 128 * k : 128 * k + 128]
        for src in range(1, N_LAYER):
            total = total + part_ref[src, :, 128 * k : 128 * k + 128]
        fields[0].append(guess_ref[0, :, at] * keep)
        fields[1].append(guess_ref[1, :, at] * keep)
        fields[2].append(thick_ref[:, at] * keep * total)
        fields[3].append(fric_ref[:, at] * ground_ref[:, at].astype(F32) * keep)
        fields[4].append(ice_ref[:, at].astype(F32) * keep)
        fields[5].append(drive_ref[0, :, at] * keep)
        fields[6].append(drive_ref[1, :, at] * keep)
    for t in range(N_TILE):
        a, b = divmod(48 + CHUNK * t, 128)
        tails = []
        for f in range(7):
            x0 = lanes_left(fields[f][a], b)
            x1 = lanes_left(fields[f][a + 1], b)
            x2 = lanes_left(fields[f][a + 2], b) if a + 2 < 5 else x1
            inner = lane < 128 - b
            out_ref[t, f] = jnp.where(inner, x0, x1)
            tails.append(jnp.where(inner, x1, x2))
        for k in range(4):
            tail = tails[2 * k]
            if 2 * k + 1 < 7:
                tail = jnp.where(lane < 56, tail, pltpu.roll(tails[2 * k + 1], 56, 1))
            out_ref[t, 7 + k] = tail


def obs_chunks_kernel(part_ref, out_ref):
    lane = lane_iota()
    for f in range(3):
        sums = []
        for k in range(4):
            total = part_ref[0, f, :, 128 * k : 128 * k + 128]
            for src in range(1, N_LAYER):
                total = total + part_ref[src, f, :, 128 * k : 128 * k + 128]
            sums.append(total)
        for t in range(N_TILE):
            a, b = divmod(24 + CHUNK * t, 128)
            x0 = lanes_left(sums[a], b)
            x1 = lanes_left(sums[a + 1], b) if a + 1 < 4 else x0
            out_ref[t, f] = jnp.where(lane < 128 - b, x0, x1)


def sweeps(coef_ref, gu_ref, gv_ref, u_ref, v_ref, n):
    def around(u, v):
        return (
            u, pltpu.roll(u, 127, 1), pltpu.roll(u, 1, 1),
            v, pltpu.roll(v, 127, 1), pltpu.roll(v, 1, 1),
        )

    def body(_, carry):
        u_first, v_first = u_ref[0], v_ref[0]
        west = around(pltpu.roll(u_ref[n - 1], 1, 0), pltpu.roll(v_ref[n - 1], 1, 0))
        here = around(u_first, v_first)
        for i in range(n):
            if i < n - 1:
                east = around(u_ref[i + 1], v_ref[i + 1])
            else:
                east = around(pltpu.roll(u_first, 7, 0), pltpu.roll(v_first, 7, 0))
            half = coef_ref[0, i]
            for own, other, base, source, ref in ((0, 3, 1, gu_ref, u_ref), (3, 0, 9, gv_ref, v_ref)):
                c = [coef_ref[base + k, i] for k in range(8)]
                a = source[i] + half * here[own]
                b = c[0] * here[own + 1] + c[1] * here[own + 2]
                d = c[2] * east[own] + c[3] * west[own]
                e = c[4] * east[other + 1] + c[5] * west[other + 1]
                g = c[6] * east[other + 2] + c[7] * west[other + 2]
                ref[i] = (a + b) + (d + (e + g))
            west, here = here, east
        return carry

    lax.fori_loop(0, SWEEPS, body, 0)


def forward_kernel(z_ref, u_out, v_out, drag_out, coef_out, flat, blk, nu_ref, coef, u_ref, v_ref, tmp):
    for f in range(7):
        flat[f, 0:128, :] = z_ref[:, f].reshape(128, 128).T
    for k in range(4):
        tail = z_ref[:, 7 + k].reshape(128, 128).T
        flat[2 * k, 128:WIDE, :] = tail[0:56]
        if 2 * k + 1 < 7:
            flat[2 * k + 1, 128:WIDE, :] = tail[56:112]
    for i in range(WB):
        u_ref[i] = flat[0, pl.ds(i, 8, stride=WB), :]
        v_ref[i] = flat[1, pl.ds(i, 8, stride=WB), :]
        for f in range(2, 7):
            blk[f - 2, i] = flat[f, pl.ds(i, 8, stride=WB), :]
    drag_out[...] = flat[3, 2 * SWEEPS : 2 * SWEEPS + CHUNK, :]
    lane = lane_iota()
    up_ok = jnp.where(lane < 127, 1.0, 0.0).astype(F32)
    down_ok = jnp.where(lane > 0, 1.0, 0.0).astype(F32)

    def up(x):
        return pltpu.roll(x, 127, 1) * up_ok

    def down(x):
        return pltpu.roll(x, 1, 1) * down_ok

    def east_of(ref, i):
        return ref[i + 1] if i < WB - 1 else pltpu.roll(ref[0], 7, 0)

    def west_of(ref, i):
        return ref[i - 1] if i > 0 else pltpu.roll(ref[WB - 1], 1, 0)

    for i in range(WB):
        u, v = u_ref[i], v_ref[i]
        ux = 0.5 * (up(u) - down(u))
        vx = 0.5 * (up(v) - down(v))
        uy = 0.5 * (east_of(u_ref, i) - west_of(u_ref, i))
        vy = 0.5 * (east_of(v_ref, i) - west_of(v_ref, i))
        shear = uy + vx
        strain = ux * ux + vy * vy + ux * vy + 0.25 * shear * shear + REGULAR
        rate = jnp.exp(jnp.log(strain) * (-1.0 / 3.0))
        nu_ref[i] = blk[0, i] * (rate * (0.5 / LAYERS))
    for i in range(WB):
        nu = nu_ref[i]
        nu_n, nu_s = up(nu), down(nu)
        nu_e, nu_w = east_of(nu_ref, i), west_of(nu_ref, i)
        drag, inside = blk[1, i], blk[2, i]
        n, s, e, w = 0.5 * (nu + nu_n), 0.5 * (nu + nu_s), 0.5 * (nu + nu_e), 0.5 * (nu + nu_w)
        rest = drag + 1.0 - inside
        q_u = 0.5 * inside / (4.0 * (n + s) + (e + w) + rest)
        q_v = 0.5 * inside / ((n + s) + 4.0 * (e + w) + rest)
        coef[0, i] = 0.5 * inside
        coef[1, i] = 4.0 * q_u * n * up_ok
        coef[2, i] = 4.0 * q_u * s * down_ok
        coef[3, i] = q_u * e
        coef[4, i] = q_u * w
        coef[5, i] = q_u * (0.5 * nu_n + 0.25 * nu_e) * up_ok
        coef[6, i] = -q_u * (0.5 * nu_n + 0.25 * nu_w) * up_ok
        coef[7, i] = -q_u * (0.5 * nu_s + 0.25 * nu_e) * down_ok
        coef[8, i] = q_u * (0.5 * nu_s + 0.25 * nu_w) * down_ok
        coef[9, i] = q_v * n * up_ok
        coef[10, i] = q_v * s * down_ok
        coef[11, i] = 4.0 * q_v * e
        coef[12, i] = 4.0 * q_v * w
        coef[13, i] = q_v * (0.5 * nu_e + 0.25 * nu_n) * up_ok
        coef[14, i] = -q_v * (0.5 * nu_w + 0.25 * nu_n) * up_ok
        coef[15, i] = -q_v * (0.5 * nu_e + 0.25 * nu_s) * down_ok
        coef[16, i] = q_v * (0.5 * nu_w + 0.25 * nu_s) * down_ok
        coef[17, i] = q_u * blk[3, i]
        coef[18, i] = q_v * blk[4, i]
        coef[19, i] = q_u
        coef[20, i] = q_v
    sweeps(coef, coef.at[17], coef.at[18], u_ref, v_ref, WB)
    for k in range(19):
        j = k if k < 17 else k + 2
        for i in range(WB):
            tmp[k % 4, pl.ds(i, 8, stride=WB), :] = coef[j, i]
        for i in range(NB):
            coef_out[k, i] = tmp[k % 4, pl.ds(SWEEPS + i, 8, stride=NB), :]
    for i in range(WB):
        flat[0, pl.ds(i, 8, stride=WB), :] = u_ref[i]
        flat[1, pl.ds(i, 8, stride=WB), :] = v_ref[i]
    u_out[...] = flat[0, SWEEPS : SWEEPS + NARROW, :]
    v_out[...] = flat[1, SWEEPS : SWEEPS + NARROW, :]


def adjoint_kernel(z_ref, u_in, v_in, drag_in, coef, out_ref, flat, u_ref, v_ref, gu_ref, gv_ref, turned):
    weight = z_ref[:, 0].reshape(128, 128).T[0:NARROW]
    flat[0] = weight * u_in[...] - z_ref[:, 1].reshape(128, 128).T[0:NARROW]
    flat[1] = weight * v_in[...] - z_ref[:, 2].reshape(128, 128).T[0:NARROW]
    for i in range(NB):
        gu_ref[i] = coef[17, i] * flat[0, pl.ds(i, 8, stride=NB), :]
        gv_ref[i] = coef[18, i] * flat[1, pl.ds(i, 8, stride=NB), :]
        u_ref[i] = jnp.zeros((8, 128), F32)
        v_ref[i] = jnp.zeros((8, 128), F32)
    sweeps(coef, gu_ref, gv_ref, u_ref, v_ref, NB)
    for i in range(NB):
        flat[0, pl.ds(i, 8, stride=NB), :] = u_ref[i]
        flat[1, pl.ds(i, 8, stride=NB), :] = v_ref[i]
    own = slice(SWEEPS, SWEEPS + CHUNK)
    u, v = u_in[own, :], v_in[own, :]
    turned[0:CHUNK, :] = u
    turned[CHUNK : 2 * CHUNK, :] = v
    turned[2 * CHUNK : 3 * CHUNK, :] = -(drag_in[...] * (u * flat[0, own, :] + v * flat[1, own, :]))
    turned[3 * CHUNK :, :] = jnp.zeros((128 - 3 * CHUNK, 128), F32)
    block = turned[...].T.reshape(N_TILE, 8, 128)
    for layer in range(N_LAYER):
        out_ref[:, layer] = block


def unpack_kernel(z_ref, vel_ref, grad_ref):
    lane = lane_iota()
    for f in range(3):
        for j in range(TILES):
            tile = None
            for chunk in range(128 * j // CHUNK, (128 * j + 127) // CHUNK + 1):
                layer, t = divmod(chunk, N_TILE)
                to = CHUNK * chunk - 128 * j
                piece = lanes_left(z_ref[t, layer], CHUNK * f - to)
                tile = piece if tile is None else jnp.where(lane >= to, piece, tile)
            if f < 2:
                vel_ref[f, :, 128 * j : 128 * j + 128] = tile
            else:
                grad_ref[:, 128 * j : 128 * j + 128] = tile


VMEM = pl.BlockSpec(memory_space=pltpu.VMEM)
SMEM = pl.BlockSpec(memory_space=pltpu.SMEM)


def call(kernel, out_shapes, scratch=(), in_specs=None, flops=0, bytes_accessed=0, **more):
    return pl.pallas_call(
        kernel,
        out_shape=[jax.ShapeDtypeStruct(s, F32) for s in out_shapes],
        in_specs=in_specs,
        out_specs=[VMEM] * len(out_shapes),
        scratch_shapes=list(scratch),
        cost_estimate=pl.CostEstimate(flops=flops, bytes_accessed=bytes_accessed, transcendentals=0),
        **more,
    )


def on_device(
    velocity_guess, hardness, thickness, friction, grounded, ice_mask, driving,
    obs_cell, obs_east, obs_north, obs_weight, obs_count,
):
    slots = (N_TILE, BLOCK)
    (packed,) = call(pack_obs_kernel, [(N_TILE, 4 * BLOCK)], in_specs=[SMEM] + [VMEM] * 4)(
        obs_count.reshape(1, N_TILE), obs_cell.reshape(slots), obs_east.reshape(slots),
        obs_north.reshape(slots), obs_weight.reshape(slots),
    )
    arrived = lax.all_to_all(packed, "tile", split_axis=0, concat_axis=0, tiled=True)
    (parts,) = call(layer_windows_kernel, [(N_LAYER, 8, 640)], in_specs=[VMEM])(hardness)
    parts = lax.all_to_all(parts, "layer", split_axis=0, concat_axis=0, tiled=True)
    (sums,) = call(
        scatter_kernel,
        [(N_LAYER, 3, 8, 512)],
        scratch=[
            pltpu.VMEM((9 * 128, BLOCK), jnp.bfloat16),
            pltpu.VMEM((TILES * ROWS, BLOCK), jnp.bfloat16),
            pltpu.VMEM((9 * 128, TILES * ROWS), F32),
        ],
        in_specs=[VMEM],
        flops=3600000000,
    )(arrived)
    sums = lax.all_to_all(sums, "layer", split_axis=0, concat_axis=0, tiled=True)
    me = lax.axis_index("layer").astype(jnp.int32).reshape(1)
    (maps,) = call(map_chunks_kernel, [(N_TILE, 11, 8, 128)], in_specs=[SMEM] + [VMEM] * 7)(
        me, parts, velocity_guess, thickness, friction, grounded, ice_mask, driving
    )
    maps = lax.all_to_all(maps, "tile", split_axis=0, concat_axis=0, tiled=True)
    (points,) = call(obs_chunks_kernel, [(N_TILE, 3, 8, 128)], in_specs=[VMEM])(sums)
    points = lax.all_to_all(points, "tile", split_axis=0, concat_axis=0, tiled=True)
    wide = (WIDE, 128)
    u, v, drag, coef = call(
        forward_kernel,
        [(NARROW, 128), (NARROW, 128), (CHUNK, 128), (19, NB, 8, 128)],
        scratch=[
            pltpu.VMEM((7,) + wide, F32),
            pltpu.VMEM((5, WB, 8, 128), F32),
            pltpu.VMEM((WB, 8, 128), F32),
            pltpu.VMEM((21, WB, 8, 128), F32),
            pltpu.VMEM((WB, 8, 128), F32),
            pltpu.VMEM((WB, 8, 128), F32),
            pltpu.VMEM((4,) + wide, F32),
        ],
        in_specs=[VMEM],
        flops=3600000000,
    )(maps)
    (shares,) = call(
        adjoint_kernel,
        [(N_TILE, N_LAYER, 8, 128)],
        scratch=[
            pltpu.VMEM((2, NARROW, 128), F32),
            pltpu.VMEM((NB, 8, 128), F32),
            pltpu.VMEM((NB, 8, 128), F32),
            pltpu.VMEM((NB, 8, 128), F32),
            pltpu.VMEM((NB, 8, 128), F32),
            pltpu.VMEM((128, 128), F32),
        ],
        in_specs=[VMEM] * 5,
        flops=3600000000,
    )(points, u, v, drag, coef)
    shares = shares.reshape(N_TILE * N_LAYER, 8, 128)
    shares = lax.all_to_all(shares, ("tile", "layer"), split_axis=0, concat_axis=0, tiled=True)
    velocity, gradient = call(unpack_kernel, [(2, 8, COLS), (8, COLS)], in_specs=[VMEM])(
        shares.reshape(N_TILE, N_LAYER, 8, 128)
    )
    return velocity, gradient


def solution(mesh):
    return jax.shard_map(
        on_device,
        mesh=mesh,
        in_specs=(
            P(None, "tile", None),
            P("layer", "tile", None),
            P("tile", None),
            P("tile", None),
            P("tile", None),
            P("tile", None),
            P(None, "tile", None),
            P("tile", "layer", None, None),
            P("tile", "layer", None, None),
            P("tile", "layer", None, None),
            P("tile", "layer", None, None),
            P("tile", "layer", None),
        ),
        out_specs=(P(None, "tile", None), P("tile", None)),
        check_vma=False,
    )
```

time: 1250 us -> 115 us (0.09)
  the two profiles are of different devices: /device:TPU:96 before, /device:TPU:1 now
where the time goes in v1:
time: 115 us; the launch traced here: 114 us
  Pallas kernels  38.7 us (34%)
  starting transfers between devices  27 us (23%)
  blocking collectives  23.2 us (20%)
  waiting for transfers between devices  20.3 us (18%)
  local copies, waits for them, and re-layouts  4.49 us (4%)
    all_to_all x1, blocking collectives, on_device(): lax.all_to_all(shares, ('tile', 'layer'), split_axis=0, concat_axis=0, ti...  23.2 us
    all_to_all x1, waiting for transfers between devices, on_device(): maps = lax.all_to_all(maps, 'tile', split_axis=0, concat_axis=0, tiled=True)  10.3 us
    pallas_call x1, Pallas kernels, on_device(): call(forward_kernel, [(NARROW, 128), (NARROW, 128), (CHUNK, 128), (19, NB...  10.2 us
    pallas_call x1, Pallas kernels, on_device(): call(scatter_kernel, [(N_LAYER, 3, 8, 512)], scratch=[pltpu.VMEM((9 * 128...  9.98 us
    all_to_all x1, starting transfers between devices, on_device(): lax.all_to_all(packed, 'tile', split_axis=0, concat_axis=0, tiled=True)  8.6 us
    pallas_call x1, Pallas kernels, on_device(): call(adjoint_kernel, [(N_TILE, N_LAYER, 8, 128)], scratch=[pltpu.VMEM((2,...  8.06 us
    all_to_all x1, starting transfers between devices, on_device(): lax.all_to_all(parts, 'layer', split_axis=0, concat_axis=0, tiled=True)  6.23 us
    all_to_all x1, waiting for transfers between devices, on_device(): lax.all_to_all(packed, 'tile', split_axis=0, concat_axis=0, tiled=True)  5.18 us
  transfers between devices with their start and end apart: 5, of which 3 were waited for; matrix products, arithmetic and copies ran while one was open for 1% of the time, Pallas kernels for 24%

profile of v1, /device:TPU:1, one launch (start us, length us, event | category | flops | bytes accessed | tf_op | source)
XLA Modules:
  0.0 114.4 jit_solution(7154577508239002825)
XLA Ops:
  0.6 1.5 %shard_map.131 = f32[16,2048]{1,0:T(8,128)} custom-call(s32[1,16]{1,0:T(1,128)} %bitcast.20, s32[16,512]{1,0:T(8,128)} %bitcast.16, f32[16,512]{1,0:T(8,128)} %bitcast.17, f32[16,512]{1,0:T(8,128)} %bitcast.18, f32[16,512]{1,0:T(8,128)} %bitcast.19), custom_call_target="tpu_custom_call" | custom-call | tf_op jit(solution)/shard_map/pallas_call | solution.py:342
  2.1 1.7 %copy.14 = f32[16,1,2048]{2,1,0:T(1,128)} copy(f32[16,1,2048]{2,0,1:T(8,128)} %bitcast.14) | data formatting | bytes 262144 | tf_op jit(solution)/shard_map/all_to_all | solution.py:346
  3.8 8.6 %all-to-all-start = ((f32[16,1,2048]{2,1,0:T(1,128)}), f32[16,1,2048]{2,1,0:T(1,128)S(1)}, u32[]{:S(2)}, u32[]{:S(2)}) async-start(f32[16,1,2048]{2,1,0:T(1,128)} %copy.14), calls=%async_computation | async-start | bytes 262144 | tf_op jit(solution)/shard_map/all_to_all | solution.py:346
  12.4 1.7 %shard_map.134 = f32[8,8,640]{2,1,0:T(8,128)} custom-call(f32[4,8,3072]{2,1,0:T(8,128)} %hard_ref.1), custom_call_target="tpu_custom_call" | custom-call | tf_op jit(solution)/shard_map/pallas_call | solution.py:347
  14.1 5.2 %all-to-all-done = f32[16,1,2048]{2,1,0:T(1,128)S(1)} async-done(((f32[16,1,2048]{2,1,0:T(1,128)}), f32[16,1,2048]{2,1,0:T(1,128)S(1)}, u32[]{:S(2)}, u32[]{:S(2)}) %all-to-all-start) | async-done | bytes 131104 | tf_op jit(solution)/shard_map/all_to_all | solution.py:346
  19.3 6.2 %all-to-all-start.3 = ((f32[8,8,640]{2,1,0:T(8,128)}), f32[8,8,640]{2,1,0:T(8,128)S(1)}, u32[]{:S(2)}, u32[]{:S(2)}) async-start(f32[8,8,640]{2,1,0:T(8,128)} %shard_map.134), calls=%async_computation.3 | async-start | bytes 327680 | tf_op jit(solution)/shard_map/all_to_all | solution.py:348
  25.5 0.7 copy.17
  26.2 10.0 %shard_map.132 = f32[8,3,8,512]{3,2,1,0:T(8,128)} custom-call(f32[16,2048]{1,0:T(8,128)} %bitcast.15), custom_call_target="tpu_custom_call" | custom-call | flops 3600000000 | tf_op jit(solution)/shard_map/pallas_call | solution.py:349
  36.2 0.0 all-to-all-done.3.part_ref
  36.2 0.0 copy-start.2
  36.2 0.7 copy-done.2
  36.9 4.8 %all-to-all-start.1 = ((f32[8,3,8,512]{3,2,1,0:T(8,128)}), f32[8,3,8,512]{3,2,1,0:T(8,128)S(1)}, u32[]{:S(2)}, u32[]{:S(2)}) async-start(f32[8,3,8,512]{3,2,1,0:T(8,128)} %shard_map.132), calls=%async_computation.1 | async-start | bytes 786432 | tf_op jit(solution)/shard_map/all_to_all | solution.py:360
  41.7 3.2 %shard_map.135 = f32[16,11,8,128]{3,2,1,0:T(8,128)} custom-call(s32[1]{0:T(128)} %bitcast.6.me_ref, f32[8,8,640]{2,1,0:T(8,128)} %copy-done.2, f32[2,8,3072]{2,1,0:T(8,128)} %guess_ref.1, f32[8,3072]{1,0:T(8,128)} %thick_ref.1, f32[8,3072]{1,0:T(8,128)} %fric_ref.1, s32[8,3072]{1,0:T(8,128)} %ground_ref.1, s32[8,3072]{1,0:T(8,128)} %ice_ref.1, ...), custom_call_target="tpu_custom_call" | custom-call | tf_op jit(solution)/shard_map/pallas_call | solution.py:362
  44.9 4.9 %all-to-all-done.1.part_ref = f32[8,3,8,512]{3,2,1,0:T(8,128)S(1)} async-done(((f32[8,3,8,512]{3,2,1,0:T(8,128)}), f32[8,3,8,512]{3,2,1,0:T(8,128)S(1)}, u32[]{:S(2)}, u32[]{:S(2)}) %all-to-all-start.1) | async-done | bytes 393248 | tf_op jit(solution)/shard_map/all_to_all | solution.py:360
  49.8 0.0 copy-start
  49.8 0.8 copy-done
  50.5 3.6 %all-to-all-start.4 = ((f32[16,11,8,128]{3,2,1,0:T(8,128)}), f32[16,11,8,128]{3,2,1,0:T(8,128)S(1)}, u32[]{:S(2)}, u32[]{:S(2)}) async-start(f32[16,11,8,128]{3,2,1,0:T(8,128)} %shard_map.135), calls=%async_computation.4 | async-start | bytes 1441792 | tf_op jit(solution)/shard_map/all_to_all | solution.py:365
  54.1 1.8 %shard_map.133 = f32[16,3,8,128]{3,2,1,0:T(8,128)} custom-call(f32[8,3,8,512]{3,2,1,0:T(8,128)} %copy-done), custom_call_target="tpu_custom_call" | custom-call | tf_op jit(solution)/shard_map/pallas_call | solution.py:366
  56.0 10.3 %all-to-all-done.4.z_ref = f32[16,11,8,128]{3,2,1,0:T(8,128)S(1)} async-done(((f32[16,11,8,128]{3,2,1,0:T(8,128)}), f32[16,11,8,128]{3,2,1,0:T(8,128)S(1)}, u32[]{:S(2)}, u32[]{:S(2)}) %all-to-all-start.4) | async-done | bytes 720928 | tf_op jit(solution)/shard_map/all_to_all | solution.py:365
  66.3 0.0 copy-start.1
  66.3 3.8 %all-to-all-start.2 = ((f32[16,3,8,128]{3,2,1,0:T(8,128)}), f32[16,3,8,128]{3,2,1,0:T(8,128)S(1)}, u32[]{:S(2)}, u32[]{:S(2)}) async-start(f32[16,3,8,128]{3,2,1,0:T(8,128)} %shard_map.133), calls=%async_computation.2 | async-start | bytes 393216 | tf_op jit(solution)/shard_map/all_to_all | solution.py:367
  70.0 0.0 copy-done.1
  70.0 10.2 %shard_map.136 = (f32[104,128]{1,0:T(8,128)}, f32[104,128]{1,0:T(8,128)}, f32[24,128]{1,0:T(8,128)}, f32[19,13,8,128]{3,2,1,0:T(8,128)}) custom-call(f32[16,11,8,128]{3,2,1,0:T(8,128)} %copy-done.1), custom_call_target="tpu_custom_call" | custom-call | flops 3600000000 | tf_op jit(solution)/shard_map/pallas_call | solution.py:369
  80.3 0.0 all-to-all-done.2.z_ref
  80.3 0.0 copy-start.3
  80.3 0.7 copy-done.3
  81.0 8.1 %shard_map.137 = f32[16,8,8,128]{3,2,1,0:T(8,128)} custom-call(f32[16,3,8,128]{3,2,1,0:T(8,128)} %copy-done.3, f32[104,128]{1,0:T(8,128)} %get-tuple-element.6.u_in, f32[104,128]{1,0:T(8,128)} %get-tuple-element.7.v_in, f32[24,128]{1,0:T(8,128)} %get-tuple-element.8.drag_in, f32[19,13,8,128]{3,2,1,0:T(8,128)} %get-tuple-element.9.coef), custom_call_target="tpu_custom_call" | custom-call | flops 3600000000 | tf_op jit(solution)/shard_map/pallas_call | solution.py:384
  89.0 23.2 %all_to_all.36 = f32[128,8,128]{2,1,0:T(8,128)} all-to-all(f32[128,8,128]{2,1,0:T(8,128)} %bitcast.13), channel_id=1, replica_groups=mesh['tile'=16,'layer'=8] {'tile','layer'}, dimensions={0} | all-to-all | bytes 1048576 | tf_op jit(solution)/shard_map/all_to_all | solution.py:399
  112.3 2.2 %shard_map.138 = (f32[2,8,3072]{2,1,0:T(8,128)}, f32[8,3072]{1,0:T(8,128)}) custom-call(f32[16,8,8,128]{3,2,1,0:T(8,128)} %bitcast.12), custom_call_target="tpu_custom_call" | custom-call | tf_op jit(solution)/shard_map/pallas_call | solution.py:400
Async XLA Ops:
  3.8 15.5 %all-to-all-start = ((f32[16,1,2048]{2,1,0:T(1,128)}), f32[16,1,2048]{2,1,0:T(1,128)S(1)}, u32[]{:S(2)}, u32[]{:S(2)}) async-start(f32[16,1,2048]{2,1,0:T(1,128)} %copy.14), calls=%async_computation | async-start | bytes 262144 | tf_op jit(solution)/shard_map/all_to_all | solution.py:346
  19.3 16.9 %all-to-all-start.3 = ((f32[8,8,640]{2,1,0:T(8,128)}), f32[8,8,640]{2,1,0:T(8,128)S(1)}, u32[]{:S(2)}, u32[]{:S(2)}) async-start(f32[8,8,640]{2,1,0:T(8,128)} %shard_map.134), calls=%async_computation.3 | async-start | bytes 327680 | tf_op jit(solution)/shard_map/all_to_all | solution.py:348
  36.2 0.7 copy-start.2
  36.9 12.9 %all-to-all-start.1 = ((f32[8,3,8,512]{3,2,1,0:T(8,128)}), f32[8,3,8,512]{3,2,1,0:T(8,128)S(1)}, u32[]{:S(2)}, u32[]{:S(2)}) async-start(f32[8,3,8,512]{3,2,1,0:T(8,128)} %shard_map.132), calls=%async_computation.1 | async-start | bytes 786432 | tf_op jit(solution)/shard_map/all_to_all | solution.py:360
  49.8 0.8 copy-start
  50.5 15.7 %all-to-all-start.4 = ((f32[16,11,8,128]{3,2,1,0:T(8,128)}), f32[16,11,8,128]{3,2,1,0:T(8,128)S(1)}, u32[]{:S(2)}, u32[]{:S(2)}) async-start(f32[16,11,8,128]{3,2,1,0:T(8,128)} %shard_map.135), calls=%async_computation.4 | async-start | bytes 1441792 | tf_op jit(solution)/shard_map/all_to_all | solution.py:365
  66.3 3.8 %copy-start.1 = (f32[16,11,8,128]{3,2,1,0:T(8,128)}, f32[16,11,8,128]{3,2,1,0:T(8,128)S(1)}, u32[]{:S(2)}) copy-start(f32[16,11,8,128]{3,2,1,0:T(8,128)S(1)} %all-to-all-done.4.z_ref) | copy-start | bytes 2162692
  66.3 14.0 %all-to-all-start.2 = ((f32[16,3,8,128]{3,2,1,0:T(8,128)}), f32[16,3,8,128]{3,2,1,0:T(8,128)S(1)}, u32[]{:S(2)}, u32[]{:S(2)}) async-start(f32[16,3,8,128]{3,2,1,0:T(8,128)} %shard_map.133), calls=%async_computation.2 | async-start | bytes 393216 | tf_op jit(solution)/shard_map/all_to_all | solution.py:367
  80.3 0.7 copy-start.3

commit v2 on v1

v2 whole, which is shorter than its diff:
```python
import jax
import jax.numpy as jnp
from jax import lax
from jax.experimental import pallas as pl
from jax.experimental.pallas import tpu as pltpu
from jax.sharding import PartitionSpec as P

SWEEPS = 40
LAYERS = 32
REGULAR = 0.01

ROWS = 8
COLS = 3072
TILES = COLS // 128
N_TILE = 16
N_LAYER = 8
BLOCK = 512
CHUNK = 24
WIDE = CHUNK + 4 * SWEEPS
NARROW = CHUNK + 2 * SWEEPS
WB = WIDE // 8
NB = NARROW // 8
SHARE = COLS // N_LAYER
F32 = jnp.float32
PACK_ROWS = 8 * 11
PIECES = 3
DEPTH = 2048
OBS_ROWS = PACK_ROWS
OBS_AT = 72


def lane_iota():
    return lax.broadcasted_iota(jnp.int32, (8, 128), 1)


def lanes_left(x, by):
    by = by % 128
    return pltpu.roll(x, 128 - by, 1) if by else x


def pack_kernel(
    me_ref, count_ref, cell_ref, east_ref, north_ref, weight_ref,
    guess_ref, fric_ref, ground_ref, ice_ref, drive_ref, out_ref,
):
    row = lax.broadcasted_iota(jnp.int32, (N_TILE, BLOCK), 0)
    slot = lax.broadcasted_iota(jnp.int32, (N_TILE, BLOCK), 1)
    count = jnp.zeros((N_TILE, BLOCK), jnp.int32)
    for d in range(N_TILE):
        count = jnp.where(row == d, count_ref[0, d], count)
    weight = jnp.where(slot < count, weight_ref[...], 0.0)
    cell = cell_ref[...]
    high = cell >> 8
    strip_row = ((cell >> 10) * 11) >> 5
    place = ((high - strip_row * (COLS // 256)) * ROWS + strip_row) * 256 + (cell & 255)
    for f, x in enumerate((place.astype(F32), weight, weight * east_ref[...], weight * north_ref[...])):
        for k in range(4):
            for half in range(2):
                at = pl.ds(8 * half * PACK_ROWS + 8 * 9 + 4 * f + k, 8, stride=PACK_ROWS)
                out_ref[at, :] = x[8 * half : 8 * half + 8, 128 * k : 128 * k + 128]

    first = 3 * me_ref[0] - 1
    lane = lane_iota()
    fields = [[] for _ in range(6)]
    for k in range(5):
        g = first + k
        keep = jnp.where(jnp.logical_and(g >= 0, g < TILES), 1.0, 0.0).astype(F32)
        at = pl.ds(pl.multiple_of(jnp.clip(g, 0, TILES - 1) * 128, 128), 128)
        fields[0].append(guess_ref[0, :, at] * keep)
        fields[1].append(guess_ref[1, :, at] * keep)
        fields[2].append(fric_ref[:, at] * ground_ref[:, at].astype(F32) * keep)
        fields[3].append(ice_ref[:, at].astype(F32) * keep)
        fields[4].append(drive_ref[0, :, at] * keep)
        fields[5].append(drive_ref[1, :, at] * keep)
    for t in range(N_TILE):
        a, b = divmod(48 + CHUNK * t, 128)
        inner = lane < 128 - b
        tails = []
        for f in range(6):
            x0 = lanes_left(fields[f][a], b)
            x1 = lanes_left(fields[f][a + 1], b)
            x2 = lanes_left(fields[f][a + 2], b) if a + 2 < 5 else x1
            out_ref[t * PACK_ROWS + 8 * f : t * PACK_ROWS + 8 * f + 8, :] = jnp.where(inner, x0, x1)
            tails.append(jnp.where(inner, x1, x2))
        for k in range(3):
            at = t * PACK_ROWS + 8 * (6 + k)
            out_ref[at : at + 8, :] = jnp.where(lane < 56, tails[2 * k], pltpu.roll(tails[2 * k + 1], 56, 1))


def stiffness_kernel(hard_ref, thick_ref, out_ref):
    for g in range(TILES):
        at = slice(128 * g, 128 * g + 128)
        part = (hard_ref[0, :, at] + hard_ref[1, :, at]) + (hard_ref[2, :, at] + hard_ref[3, :, at])
        out_ref[:, at] = thick_ref[:, at] * part


def scatter_kernel(obs_ref, stiff_ref, out_ref, lhs_ref, rhs_ref, acc_ref):
    acc_ref[...] = jnp.zeros_like(acc_ref)
    step16 = lax.broadcasted_iota(jnp.int32, (16, 128), 0).astype(F32).astype(jnp.bfloat16)
    zero16 = jnp.zeros((16, 128), jnp.bfloat16)
    one16 = jnp.ones((16, 128), jnp.bfloat16)

    def rows(x):
        return jnp.broadcast_to(x, (16, 128)).astype(jnp.bfloat16)

    def body(step, carry):
        for q in range(DEPTH // 128):
            lanes = slice(128 * q, 128 * q + 128)
            base = (step * (DEPTH // BLOCK) + q // 4) * OBS_ROWS + OBS_AT + q % 4
            place = obs_ref[pl.ds(base, 1), :].astype(jnp.int32)
            high = rows((place >> 8).astype(F32))
            low = rows((place & 255).astype(F32))
            pieces = []
            for f in range(3):
                value = obs_ref[pl.ds(base + 4 * (f + 1), 1), :]
                for k in range(PIECES):
                    piece = value.astype(jnp.bfloat16).astype(F32)
                    pieces.append(rows(piece))
                    if k < PIECES - 1:
                        value = value - piece
            for b in range(16):
                rhs_ref[16 * b : 16 * b + 16, lanes] = jnp.where(low == step16 + 16.0 * b, one16, zero16)
            for b in range(6):
                hit = high == step16 + 16.0 * b
                for k in range(3 * PIECES):
                    lhs_ref[k * 96 + 16 * b : k * 96 + 16 * b + 16, lanes] = jnp.where(hit, pieces[k], zero16)
        acc_ref[...] += lax.dot_general(
            lhs_ref[...], rhs_ref[...], (((1,), (1,)), ((), ())), preferred_element_type=F32
        )
        return carry

    lax.fori_loop(0, N_TILE * BLOCK // DEPTH, body, 0)
    lane = lane_iota()
    zero = jnp.zeros((8, 128), F32)

    def windows(tiles, shift, count):
        turned = [lanes_left(x, shift) for x in tiles]
        pick = lambda g: turned[g] if 0 <= g < TILES else zero
        return [
            [jnp.where(lane < 128 - shift, pick(3 * dest - 1 + k), pick(3 * dest + k)) for k in range(count)]
            for dest in range(N_LAYER)
        ]

    stiff = windows([stiff_ref[:, 128 * g : 128 * g + 128] for g in range(TILES)], 48, 5)
    for f in range(3):
        total = acc_ref[PIECES * f * 96 : PIECES * f * 96 + 96, :]
        for k in range(1, PIECES):
            total = total + acc_ref[(PIECES * f + k) * 96 : (PIECES * f + k + 1) * 96, :]
        tiles = [total[8 * (g // 2) : 8 * (g // 2) + 8, 128 * (g % 2) : 128 * (g % 2) + 128] for g in range(TILES)]
        sums = windows(tiles, 88, 4)
        for dest in range(N_LAYER):
            for k in range(4):
                tile = sums[dest][k]
                if f == 0 and k == 3:
                    tile = jnp.where(lane < 80, tile, pltpu.roll(stiff[dest][4], 80, 1))
                out_ref[dest, 4 + 4 * f + k] = tile
    for dest in range(N_LAYER):
        for k in range(4):
            out_ref[dest, k] = stiff[dest][k]


def chunks_kernel(part_ref, out_ref):
    lane = lane_iota()

    def summed(k):
        total = part_ref[0, k]
        for src in range(1, N_LAYER):
            total = total + part_ref[src, k]
        return total

    tiles = [summed(k) for k in range(16)]
    stiff = tiles[0:4] + [lanes_left(tiles[7], 80)]
    for t in range(N_TILE):
        a, b = divmod(CHUNK * t, 128)
        inner = lane < 128 - b
        for f in range(4):
            x = stiff if f == 0 else tiles[4 * f : 4 * f + 4]
            x0 = lanes_left(x[a], b)
            x1 = lanes_left(x[a + 1], b) if a + 1 < len(x) else x0
            out_ref[t, f] = jnp.where(inner, x0, x1)
            if f == 0:
                x2 = lanes_left(x[a + 2], b) if a + 2 < 5 else x1
                out_ref[t, 4] = jnp.where(inner, x1, x2)


def put_state(ref, i, u, v):
    for at, x in ((0, u), (3, v)):
        ref[at, i] = x
        ref[at + 1, i] = pltpu.roll(x, 127, 1)
        ref[at + 2, i] = pltpu.roll(x, 1, 1)


def sweep(coef_ref, gu_ref, gv_ref, old, new, n, start):
    def west_side(i):
        return [old[k, i - 1] if i > 0 else pltpu.roll(old[k, n - 1], 1, 0) for k in range(6)]

    west = west_side(start)
    here = [old[k, start] for k in range(6)]
    for step in range(n):
        i = (start + step) % n
        if step and i == 0:
            west = west_side(0)
            here = [old[k, 0] for k in range(6)]
        east = [old[k, i + 1] if i < n - 1 else pltpu.roll(old[k, 0], 7, 0) for k in range(6)]
        half = coef_ref[0, i]
        fresh = []
        for own, other, base, source in ((0, 3, 1, gu_ref), (3, 0, 9, gv_ref)):
            c = [coef_ref[base + k, i] for k in range(8)]
            a = source[i] + half * here[own]
            b = c[0] * here[own + 1] + c[1] * here[own + 2]
            d = c[2] * east[own] + c[3] * west[own]
            e = c[4] * east[other + 1] + c[5] * west[other + 1]
            g = c[6] * east[other + 2] + c[7] * west[other + 2]
            fresh.append((a + b) + (d + (e + g)))
        put_state(new, i, *fresh)
        west, here = here, east


def sweeps(coef_ref, gu_ref, gv_ref, one, two, n):
    def body(_, carry):
        sweep(coef_ref, gu_ref, gv_ref, one, two, n, 0)
        sweep(coef_ref, gu_ref, gv_ref, two, one, n, n // 2)
        return carry

    lax.fori_loop(0, SWEEPS // 2, body, 0)


def up_down():
    lane = lane_iota()
    up_ok = jnp.where(lane < 127, 1.0, 0.0).astype(F32)
    down_ok = jnp.where(lane > 0, 1.0, 0.0).astype(F32)
    return up_ok, down_ok, lambda x: pltpu.roll(x, 127, 1) * up_ok, lambda x: pltpu.roll(x, 1, 1) * down_ok


def east_of(ref, i):
    return ref[i + 1] if i < WB - 1 else pltpu.roll(ref[0], 7, 0)


def west_of(ref, i):
    return ref[i - 1] if i > 0 else pltpu.roll(ref[WB - 1], 1, 0)


def prepare_kernel(x_ref, blk, flat):
    def tile(k):
        return jnp.concatenate(
            [x_ref[t * PACK_ROWS + 8 * k : t * PACK_ROWS + 8 * k + 8, :] for t in range(N_TILE)], 0
        ).T

    for f in range(6):
        flat[f, 0:128, :] = tile(f)
    for k in range(3):
        tail = tile(6 + k)
        flat[2 * k, 128:WIDE, :] = tail[0:56]
        flat[2 * k + 1, 128:WIDE, :] = tail[56:112]
    for f in range(6):
        for i in range(WB):
            blk[f, i] = flat[f, pl.ds(i, 8, stride=WB), :]
    _, _, up, down = up_down()
    u_ref, v_ref = blk.at[0], blk.at[1]
    for i in range(WB):
        u, v = u_ref[i], v_ref[i]
        ux = 0.5 * (up(u) - down(u))
        vx = 0.5 * (up(v) - down(v))
        uy = 0.5 * (east_of(u_ref, i) - west_of(u_ref, i))
        vy = 0.5 * (east_of(v_ref, i) - west_of(v_ref, i))
        shear = uy + vx
        strain = ux * ux + vy * vy + ux * vy + 0.25 * shear * shear + REGULAR
        blk[6, i] = jnp.exp(jnp.log(strain) * (-1.0 / 3.0)) * (0.5 / LAYERS)


def solve_kernel(
    z_ref, blk, out_ref, flat, nu_ref, coef, wide_a, wide_b, tmp, near, near_a, near_b, gu_ref, gv_ref, turned
):
    def tile(k):
        return z_ref[:, k].reshape(128, 128).T

    flat[0, 0:128, :] = tile(0)
    flat[0, 128:WIDE, :] = tile(4)[0:56]
    up_ok, down_ok, up, down = up_down()
    for i in range(WB):
        put_state(wide_a, i, blk[0, i], blk[1, i])
        nu_ref[i] = blk[6, i] * flat[0, pl.ds(i, 8, stride=WB), :]
    for i in range(WB):
        nu = nu_ref[i]
        nu_n, nu_s = up(nu), down(nu)
        nu_e, nu_w = east_of(nu_ref, i), west_of(nu_ref, i)
        drag, inside = blk[2, i], blk[3, i]
        n, s, e, w = 0.5 * (nu + nu_n), 0.5 * (nu + nu_s), 0.5 * (nu + nu_e), 0.5 * (nu + nu_w)
        rest = drag + 1.0 - inside
        q_u = 0.5 * inside / (4.0 * (n + s) + (e + w) + rest)
        q_v = 0.5 * inside / ((n + s) + 4.0 * (e + w) + rest)
        coef[0, i] = 0.5 * inside
        coef[1, i] = 4.0 * q_u * n * up_ok
        coef[2, i] = 4.0 * q_u * s * down_ok
        coef[3, i] = q_u * e
        coef[4, i] = q_u * w
        coef[5, i] = q_u * (0.5 * nu_n + 0.25 * nu_e) * up_ok
        coef[6, i] = -q_u * (0.5 * nu_n + 0.25 * nu_w) * up_ok
        coef[7, i] = -q_u * (0.5 * nu_s + 0.25 * nu_e) * down_ok
        coef[8, i] = q_u * (0.5 * nu_s + 0.25 * nu_w) * down_ok
        coef[9, i] = q_v * n * up_ok
        coef[10, i] = q_v * s * down_ok
        coef[11, i] = 4.0 * q_v * e
        coef[12, i] = 4.0 * q_v * w
        coef[13, i] = q_v * (0.5 * nu_e + 0.25 * nu_n) * up_ok
        coef[14, i] = -q_v * (0.5 * nu_w + 0.25 * nu_n) * up_ok
        coef[15, i] = -q_v * (0.5 * nu_e + 0.25 * nu_s) * down_ok
        coef[16, i] = q_v * (0.5 * nu_w + 0.25 * nu_s) * down_ok
        coef[17, i] = q_u * blk[4, i]
        coef[18, i] = q_v * blk[5, i]
        coef[19, i] = q_u
        coef[20, i] = q_v
    for k in range(19):
        j = k if k < 17 else k + 2
        for i in range(WB):
            tmp[k % 4, pl.ds(i, 8, stride=WB), :] = coef[j, i]
        for i in range(NB):
            near[k, i] = tmp[k % 4, pl.ds(SWEEPS + i, 8, stride=NB), :]
    sweeps(coef, coef.at[17], coef.at[18], wide_a, wide_b, WB)
    for i in range(WB):
        flat[0, pl.ds(i, 8, stride=WB), :] = wide_a[0, i]
        flat[1, pl.ds(i, 8, stride=WB), :] = wide_a[3, i]
        flat[2, pl.ds(i, 8, stride=WB), :] = blk[2, i]
    weight = tile(1)[0:NARROW]
    span = slice(SWEEPS, SWEEPS + NARROW)
    tmp[0, 0:NARROW, :] = weight * flat[0, span, :] - tile(2)[0:NARROW]
    tmp[1, 0:NARROW, :] = weight * flat[1, span, :] - tile(3)[0:NARROW]
    for i in range(NB):
        gu_ref[i] = near[17, i] * tmp[0, pl.ds(i, 8, stride=NB), :]
        gv_ref[i] = near[18, i] * tmp[1, pl.ds(i, 8, stride=NB), :]
        for k in range(6):
            near_a[k, i] = jnp.zeros((8, 128), F32)
    sweeps(near, gu_ref, gv_ref, near_a, near_b, NB)
    for i in range(NB):
        tmp[0, pl.ds(i, 8, stride=NB), :] = near_a[0, i]
        tmp[1, pl.ds(i, 8, stride=NB), :] = near_a[3, i]
    own = slice(2 * SWEEPS, 2 * SWEEPS + CHUNK)
    mine = slice(SWEEPS, SWEEPS + CHUNK)
    u, v, drag = flat[0, own, :], flat[1, own, :], flat[2, own, :]
    turned[0:CHUNK, :] = u
    turned[CHUNK : 2 * CHUNK, :] = v
    turned[2 * CHUNK : 3 * CHUNK, :] = -(drag * (u * tmp[0, mine, :] + v * tmp[1, mine, :]))
    turned[3 * CHUNK :, :] = jnp.zeros((128 - 3 * CHUNK, 128), F32)
    block = turned[...].T.reshape(N_TILE, 8, 128)
    for layer in range(N_LAYER):
        out_ref[:, layer] = block


def unpack_kernel(z_ref, vel_ref, grad_ref):
    lane = lane_iota()
    for f in range(3):
        for j in range(TILES):
            tile = None
            for chunk in range(128 * j // CHUNK, (128 * j + 127) // CHUNK + 1):
                layer, t = divmod(chunk, N_TILE)
                to = CHUNK * chunk - 128 * j
                piece = lanes_left(z_ref[t, layer], CHUNK * f - to)
                tile = piece if tile is None else jnp.where(lane >= to, piece, tile)
            if f < 2:
                vel_ref[f, :, 128 * j : 128 * j + 128] = tile
            else:
                grad_ref[:, 128 * j : 128 * j + 128] = tile


VMEM = pl.BlockSpec(memory_space=pltpu.VMEM)
SMEM = pl.BlockSpec(memory_space=pltpu.SMEM)


def call(kernel, out_shapes, scratch=(), in_specs=None, flops=1000000, limit=8):
    return pl.pallas_call(
        kernel,
        out_shape=[jax.ShapeDtypeStruct(s, F32) for s in out_shapes],
        in_specs=in_specs,
        out_specs=[VMEM] * len(out_shapes),
        scratch_shapes=list(scratch),
        cost_estimate=pl.CostEstimate(flops=flops, bytes_accessed=1000000, transcendentals=0),
        compiler_params=pltpu.CompilerParams(vmem_limit_bytes=limit << 20),
    )


def exchange(x, axis):
    return lax.all_to_all(x, axis, split_axis=0, concat_axis=0, tiled=True)


def on_device(
    velocity_guess, hardness, thickness, friction, grounded, ice_mask, driving,
    obs_cell, obs_east, obs_north, obs_weight, obs_count,
):
    slots = (N_TILE, BLOCK)
    me = lax.axis_index("layer").astype(jnp.int32).reshape(1)
    (packed,) = call(pack_kernel, [(N_TILE * PACK_ROWS, 128)], in_specs=[SMEM] * 2 + [VMEM] * 9, limit=58)(
        me, obs_count.reshape(1, N_TILE), obs_cell.reshape(slots), obs_east.reshape(slots),
        obs_north.reshape(slots), obs_weight.reshape(slots),
        velocity_guess, friction, grounded, ice_mask, driving,
    )
    arrived = exchange(packed.reshape(N_TILE, PACK_ROWS, 128), "tile").reshape(N_TILE * PACK_ROWS, 128)
    (stiff,) = call(stiffness_kernel, [(8, COLS)], in_specs=[VMEM] * 2)(hardness, thickness)
    (parts,) = call(
        scatter_kernel,
        [(N_LAYER, 16, 8, 128)],
        scratch=[
            pltpu.VMEM((3 * PIECES * 96, DEPTH), jnp.bfloat16),
            pltpu.VMEM((256, DEPTH), jnp.bfloat16),
            pltpu.VMEM((3 * PIECES * 96, 256), F32),
        ],
        in_specs=[VMEM] * 2,
        flops=3600000000,
        limit=16,
    )(arrived, stiff)
    parts = exchange(parts, "layer")
    (blocks,) = call(
        prepare_kernel, [(7, WB, 8, 128)], scratch=[pltpu.VMEM((6, WIDE, 128), F32)], in_specs=[VMEM]
    )(arrived)
    (chunks,) = call(chunks_kernel, [(N_TILE, 5, 8, 128)], in_specs=[VMEM])(parts)
    chunks = exchange(chunks, "tile")
    (shares,) = call(
        solve_kernel,
        [(N_TILE, N_LAYER, 8, 128)],
        scratch=[
            pltpu.VMEM((3, WIDE, 128), F32),
            pltpu.VMEM((WB, 8, 128), F32),
            pltpu.VMEM((21, WB, 8, 128), F32),
            pltpu.VMEM((6, WB, 8, 128), F32),
            pltpu.VMEM((6, WB, 8, 128), F32),
            pltpu.VMEM((4, WIDE, 128), F32),
            pltpu.VMEM((19, NB, 8, 128), F32),
            pltpu.VMEM((6, NB, 8, 128), F32),
            pltpu.VMEM((6, NB, 8, 128), F32),
            pltpu.VMEM((NB, 8, 128), F32),
            pltpu.VMEM((NB, 8, 128), F32),
            pltpu.VMEM((128, 128), F32),
        ],
        in_specs=[VMEM] * 2,
        flops=3600000000,
        limit=16,
    )(chunks, blocks)
    shares = exchange(shares.reshape(N_TILE * N_LAYER, 8, 128), ("tile", "layer"))
    velocity, gradient = call(unpack_kernel, [(2, 8, COLS), (8, COLS)], in_specs=[VMEM])(
        shares.reshape(N_TILE, N_LAYER, 8, 128)
    )
    return velocity, gradient


def solution(mesh):
    return jax.shard_map(
        on_device,
        mesh=mesh,
        in_specs=(
            P(None, "tile", None),
            P("layer", "tile", None),
            P("tile", None),
            P("tile", None),
            P("tile", None),
            P("tile", None),
            P(None, "tile", None),
            P("tile", "layer", None, None),
            P("tile", "layer", None, None),
            P("tile", "layer", None, None),
            P("tile", "layer", None, None),
            P("tile", "layer", None),
        ),
        out_specs=(P(None, "tile", None), P("tile", None)),
        check_vma=False,
    )
```

time: 115 us -> 91.9 us (0.80)
  Pallas kernels: 38.7 us -> 23.6 us
  starting transfers between devices: 27 us -> 12.3 us
  blocking collectives: 23.2 us -> 35.5 us
  local copies, waits for them, and re-layouts: 4.49 us -> 0.01 us
    all_to_all x5 -> x2, starting transfers between devices: 27 us -> 12.3 us  [exchange(): return lax.all_to_all(x, axis, split_axis=0, concat_axis=0, tiled=True)]
    pallas_call x7 -> x6, Pallas kernels: 36.5 us -> 22.5 us  [the longest x1 12.8 us: on_device(): call(solve_kernel, [(N_TILE, N_LAYER, 8, 128)], scratch=[pltpu.VMEM((3, W...]
    all_to_all x1 -> x2, blocking collectives: 23.2 us -> 35.5 us  [exchange(): return lax.all_to_all(x, axis, split_axis=0, concat_axis=0, tiled=True)]
    unnamed x9 -> x4, local copies, waits for them, and re-layouts: 2.8 us -> 0.01 us
    all_to_all x1 -> x0, local copies, waits for them, and re-layouts: 1.69 us -> none  [on_device(): lax.all_to_all(packed, 'tile', split_axis=0, concat_axis=0, tiled=True)]
    all_to_all x5 -> x2, waiting for transfers between devices: 20.3 us -> 19.4 us  [exchange(): return lax.all_to_all(x, axis, split_axis=0, concat_axis=0, tiled=True)]
  transfers between devices with their start and end apart: 5 -> 2, of which waited for: 3 -> 2; matrix products, arithmetic and copies ran while one was open for 1% -> 0% of each run, Pallas kernels for 24% -> 0%
where the time goes in v2:
time: 91.9 us; the launch traced here: 91.5 us
  blocking collectives  35.5 us (39%)
  Pallas kernels  23.6 us (26%)
  waiting for transfers between devices  19.4 us (21%)
  starting transfers between devices  12.3 us (13%)
    all_to_all x2, blocking collectives, exchange(): return lax.all_to_all(x, axis, split_axis=0, concat_axis=0, tiled=True)  35.5 us
    all_to_all x2, waiting for transfers between devices, exchange(): return lax.all_to_all(x, axis, split_axis=0, concat_axis=0, tiled=True)  19.4 us
    pallas_call x1, Pallas kernels, on_device(): call(solve_kernel, [(N_TILE, N_LAYER, 8, 128)], scratch=[pltpu.VMEM((3, W...  12.8 us
    all_to_all x2, starting transfers between devices, exchange(): return lax.all_to_all(x, axis, split_axis=0, concat_axis=0, tiled=True)  12.3 us
    pallas_call x1, Pallas kernels, on_device(): call(scatter_kernel, [(N_LAYER, 16, 8, 128)], scratch=[pltpu.VMEM((3 * PI...  5.21 us
    pallas_call x1, Pallas kernels, on_device(): call(pack_kernel, [(N_TILE * PACK_ROWS, 128)], in_specs=[SMEM] * 2 + [VME...  3.11 us
  transfers between devices with their start and end apart: 2, of which 2 were waited for; matrix products, arithmetic and copies ran while one was open for 0% of the time, Pallas kernels for 0%

profile of v2, /device:TPU:1, one launch (start us, length us, event | category | flops | bytes accessed | tf_op | source)
XLA Modules:
  0.0 91.5 jit_solution(10732446201784397306)
XLA Ops:
  0.6 3.1 %shard_map.131 = f32[1408,128]{1,0:T(8,128)} custom-call(s32[1]{0:T(128)} %bitcast.me_ref, s32[1,16]{1,0:T(1,128)} %bitcast.19, s32[16,512]{1,0:T(8,128)} %bitcast.15, f32[16,512]{1,0:T(8,128)} %bitcast.16, f32[16,512]{1,0:T(8,128)} %bitcast.17, f32[16,512]{1,0:T(8,128)} %bitcast.18, f32[2,8,3072]{2,1,0:T(8,128)} %guess_ref.1, f32[8,3072]{1,0:T(8,128)} %fric_ref.1, ...), custom_call_target="tpu_custom_call" | custom-call | flops 1000000 | bytes 1000000 | tf_op jit(solution)/shard_map/pallas_call | solution.py:390
  3.7 0.0 copy-start
  3.7 0.0 copy-start.1
  3.7 8.7 %all-to-all-start = ((f32[16,88,128]{2,1,0:T(8,128)}), f32[16,88,128]{2,1,0:T(8,128)S(1)}, u32[]{:S(2)}, u32[]{:S(2)}) async-start(f32[16,88,128]{2,1,0:T(8,128)} %bitcast.14), calls=%async_computation | async-start | bytes 1441792 | tf_op jit(solution)/shard_map/all_to_all | solution.py:381
  12.5 0.0 copy-done
  12.5 0.0 copy-done.1
  12.5 12.1 %all-to-all-done = f32[16,88,128]{2,1,0:T(8,128)S(1)} async-done(((f32[16,88,128]{2,1,0:T(8,128)}), f32[16,88,128]{2,1,0:T(8,128)S(1)}, u32[]{:S(2)}, u32[]{:S(2)}) %all-to-all-start) | async-done | bytes 720928 | tf_op jit(solution)/shard_map/all_to_all | solution.py:381
  24.7 5.2 %shard_map.133 = f32[8,16,8,128]{3,2,1,0:T(8,128)S(1)} custom-call(f32[1408,128]{1,0:T(8,128)S(1)} %bitcast.10, f32[8,3072]{1,0:T(8,128)S(1)} %shard_map.132.stiff_ref), custom_call_target="tpu_custom_call" | custom-call | flops 3600000000 | bytes 1000000 | tf_op jit(solution)/shard_map/pallas_call | solution.py:397
  29.9 15.8 %all_to_all.20.part_ref = f32[8,16,8,128]{3,2,1,0:T(8,128)S(1)} all-to-all(f32[8,16,8,128]{3,2,1,0:T(8,128)S(1)} %shard_map.133), channel_id=1, replica_groups=mesh['tile'=16,'layer'=8] {'layer'}, dimensions={0} | all-to-all | bytes 1048576 | tf_op jit(solution)/shard_map/all_to_all | solution.py:381
  45.7 0.9 %shard_map.134 = f32[16,5,8,128]{3,2,1,0:T(8,128)} custom-call(f32[8,16,8,128]{3,2,1,0:T(8,128)S(1)} %all_to_all.20.part_ref), custom_call_target="tpu_custom_call" | custom-call | flops 1000000 | bytes 1000000 | tf_op jit(solution)/shard_map/pallas_call | solution.py:413
  46.7 3.5 %all-to-all-start.2 = ((f32[16,5,8,128]{3,2,1,0:T(8,128)}), f32[16,5,8,128]{3,2,1,0:T(8,128)S(1)}, u32[]{:S(2)}, u32[]{:S(2)}) async-start(f32[16,5,8,128]{3,2,1,0:T(8,128)} %shard_map.134), calls=%async_computation.2 | async-start | bytes 655360 | tf_op jit(solution)/shard_map/all_to_all | solution.py:381
  50.2 0.4 shard_map.135.blk
  50.6 7.3 %all-to-all-done.2.z_ref = f32[16,5,8,128]{3,2,1,0:T(8,128)S(1)} async-done(((f32[16,5,8,128]{3,2,1,0:T(8,128)}), f32[16,5,8,128]{3,2,1,0:T(8,128)S(1)}, u32[]{:S(2)}, u32[]{:S(2)}) %all-to-all-start.2) | async-done | bytes 327712 | tf_op jit(solution)/shard_map/all_to_all | solution.py:381
  57.9 12.8 %shard_map.136 = f32[16,8,8,128]{3,2,1,0:T(8,128)S(1)} custom-call(f32[16,5,8,128]{3,2,1,0:T(8,128)S(1)} %all-to-all-done.2.z_ref, f32[7,23,8,128]{3,2,1,0:T(8,128)S(1)} %shard_map.135.blk), custom_call_target="tpu_custom_call" | custom-call | flops 3600000000 | bytes 1000000 | tf_op jit(solution)/shard_map/pallas_call | solution.py:415
  70.7 19.7 %all_to_all.21 = f32[128,8,128]{2,1,0:T(8,128)S(1)} all-to-all(f32[128,8,128]{2,1,0:T(8,128)S(1)} %bitcast.13), channel_id=1, replica_groups=mesh['tile'=16,'layer'=8] {'tile','layer'}, dimensions={0} | all-to-all | bytes 1048576 | tf_op jit(solution)/shard_map/all_to_all | solution.py:381
  90.3 1.1 %shard_map.137 = (f32[2,8,3072]{2,1,0:T(8,128)}, f32[8,3072]{1,0:T(8,128)}) custom-call(f32[16,8,8,128]{3,2,1,0:T(8,128)S(1)} %bitcast.12), custom_call_target="tpu_custom_call" | custom-call | flops 1000000 | bytes 1000000 | tf_op jit(solution)/shard_map/pallas_call | solution.py:437
  (1 shorter events, 0.0 us)
Async XLA Ops:
  3.7 8.7 %copy-start = (f32[4,8,3072]{2,1,0:T(8,128)S(1)}, f32[4,8,3072]{2,1,0:T(8,128)}, u32[]{:S(2)}) copy-start(f32[4,8,3072]{2,1,0:T(8,128)} %hard_ref.1) | copy-start | bytes 1179652
  3.7 8.8 %copy-start.1 = (f32[8,3072]{1,0:T(8,128)S(1)}, f32[8,3072]{1,0:T(8,128)}, u32[]{:S(2)}) copy-start(f32[8,3072]{1,0:T(8,128)} %thick_ref.1) | copy-start | bytes 294916
  3.7 20.9 %all-to-all-start = ((f32[16,88,128]{2,1,0:T(8,128)}), f32[16,88,128]{2,1,0:T(8,128)S(1)}, u32[]{:S(2)}, u32[]{:S(2)}) async-start(f32[16,88,128]{2,1,0:T(8,128)} %bitcast.14), calls=%async_computation | async-start | bytes 1441792 | tf_op jit(solution)/shard_map/all_to_all | solution.py:381
  46.7 11.3 %all-to-all-start.2 = ((f32[16,5,8,128]{3,2,1,0:T(8,128)}), f32[16,5,8,128]{3,2,1,0:T(8,128)S(1)}, u32[]{:S(2)}, u32[]{:S(2)}) async-start(f32[16,5,8,128]{3,2,1,0:T(8,128)} %shard_map.134), calls=%async_computation.2 | async-start | bytes 655360 | tf_op jit(solution)/shard_map/all_to_all | solution.py:381

commit v3 on v2

--- a/solution.py
+++ b/solution.py
@@ -93,7 +93,8 @@
         out_ref[:, at] = thick_ref[:, at] * part
 
 
-def scatter_kernel(obs_ref, stiff_ref, out_ref, lhs_ref, rhs_ref, acc_ref):
+def scatter_kernel(me_ref, obs_ref, stiff_ref, *refs):
+    outs, (lhs_ref, rhs_ref, acc_ref, turned_ref) = refs[:N_LAYER], refs[N_LAYER:]
     acc_ref[...] = jnp.zeros_like(acc_ref)
     step16 = lax.broadcasted_iota(jnp.int32, (16, 128), 0).astype(F32).astype(jnp.bfloat16)
     zero16 = jnp.zeros((16, 128), jnp.bfloat16)
@@ -132,39 +133,36 @@
     lane = lane_iota()
     zero = jnp.zeros((8, 128), F32)
 
-    def windows(tiles, shift, count):
-        turned = [lanes_left(x, shift) for x in tiles]
-        pick = lambda g: turned[g] if 0 <= g < TILES else zero
-        return [
-            [jnp.where(lane < 128 - shift, pick(3 * dest - 1 + k), pick(3 * dest + k)) for k in range(count)]
-            for dest in range(N_LAYER)
-        ]
-
-    stiff = windows([stiff_ref[:, 128 * g : 128 * g + 128] for g in range(TILES)], 48, 5)
+    def turn(f, tiles, shift):
+        turned = [zero] + [lanes_left(x, shift) for x in tiles] + [zero, zero]
+        for g in range(TILES + 2):
+            turned_ref[f, g] = jnp.where(lane < 128 - shift, turned[g], turned[g + 1])
+
+    turn(0, [stiff_ref[:, 128 * g : 128 * g + 128] for g in range(TILES)], 48)
     for f in range(3):
         total = acc_ref[PIECES * f * 96 : PIECES * f * 96 + 96, :]
         for k in range(1, PIECES):
             total = total + acc_ref[(PIECES * f + k) * 96 : (PIECES * f + k + 1) * 96, :]
         tiles = [total[8 * (g // 2) : 8 * (g // 2) + 8, 128 * (g % 2) : 128 * (g % 2) + 128] for g in range(TILES)]
-        sums = windows(tiles, 88, 4)
-        for dest in range(N_LAYER):
+        turn(f + 1, tiles, 88)
+    for d in range(N_LAYER):
+        first = 3 * ((me_ref[0] + d) & (N_LAYER - 1))
+        for f in range(4):
             for k in range(4):
-                tile = sums[dest][k]
-                if f == 0 and k == 3:
-                    tile = jnp.where(lane < 80, tile, pltpu.roll(stiff[dest][4], 80, 1))
-                out_ref[dest, 4 + 4 * f + k] = tile
-    for dest in range(N_LAYER):
-        for k in range(4):
-            out_ref[dest, k] = stiff[dest][k]
-
-
-def chunks_kernel(part_ref, out_ref):
+                tile = turned_ref[f, first + k]
+                if f == 1 and k == 3:
+                    tile = jnp.where(lane < 80, tile, pltpu.roll(turned_ref[0, first + 4], 80, 1))
+                outs[d][4 * f + k] = tile
+
+
+def chunks_kernel(*refs):
+    parts, out_ref = refs[:N_LAYER], refs[N_LAYER]
     lane = lane_iota()
 
     def summed(k):
-        total = part_ref[0, k]
-        for src in range(1, N_LAYER):
-            total = total + part_ref[src, k]
+        total = parts[0][k]
+        for part in parts[1:]:
+            total = total + part[k]
         return total
 
     tiles = [summed(k) for k in range(16)]
@@ -172,14 +170,17 @@
     for t in range(N_TILE):
         a, b = divmod(CHUNK * t, 128)
         inner = lane < 128 - b
-        for f in range(4):
-            x = stiff if f == 0 else tiles[4 * f : 4 * f + 4]
+        x0 = lanes_left(stiff[a], b)
+        x1 = lanes_left(stiff[a + 1], b)
+        x2 = lanes_left(stiff[a + 2], b) if a + 2 < 5 else x1
+        out_ref[t, 0] = jnp.where(inner, x0, x1)
+        tail = jnp.where(inner, x1, x2)
+        for f in range(1, 4):
+            x = tiles[4 * f : 4 * f + 4]
             x0 = lanes_left(x[a], b)
-            x1 = lanes_left(x[a + 1], b) if a + 1 < len(x) else x0
-            out_ref[t, f] = jnp.where(inner, x0, x1)
-            if f == 0:
-                x2 = lanes_left(x[a + 2], b) if a + 2 < 5 else x1
-                out_ref[t, 4] = jnp.where(inner, x1, x2)
+            x1 = lanes_left(x[a + 1], b) if a + 1 < 4 else x0
+            rest = pltpu.roll(tail, NARROW - CHUNK * (f - 1), 1)
+            out_ref[t, f] = jnp.where(lane < NARROW, jnp.where(inner, x0, x1), rest)
 
 
 def put_state(ref, i, u, v):
@@ -274,7 +275,10 @@
         return z_ref[:, k].reshape(128, 128).T
 
     flat[0, 0:128, :] = tile(0)
-    flat[0, 128:WIDE, :] = tile(4)[0:56]
+    for f in range(1, 4):
+        size = min(CHUNK, WIDE - 128 - CHUNK * (f - 1))
+        at = 128 + CHUNK * (f - 1)
+        flat[0, at : at + size, :] = tile(f)[NARROW : NARROW + size]
     up_ok, down_ok, up, down = up_down()
     for i in range(WB):
         put_state(wide_a, i, blk[0, i], blk[1, i])
@@ -340,20 +344,38 @@
     turned[CHUNK : 2 * CHUNK, :] = v
     turned[2 * CHUNK : 3 * CHUNK, :] = -(drag * (u * tmp[0, mine, :] + v * tmp[1, mine, :]))
     turned[3 * CHUNK :, :] = jnp.zeros((128 - 3 * CHUNK, 128), F32)
-    block = turned[...].T.reshape(N_TILE, 8, 128)
-    for layer in range(N_LAYER):
-        out_ref[:, layer] = block
-
-
-def unpack_kernel(z_ref, vel_ref, grad_ref):
+    tmp[0, 0:128, :] = turned[...].T
+    lane = lax.broadcasted_iota(jnp.int32, (N_TILE, 128), 1)
+    pieces = [tmp[0, pl.ds(r, N_TILE, stride=8), :] for r in range(8)]
+    for k in range(5):
+        row = None
+        for r in range(8):
+            to = 3 * CHUNK * r - 128 * k
+            if -3 * CHUNK < to < 128:
+                piece = pltpu.roll(pieces[r], to % 128, 1) if to % 128 else pieces[r]
+                row = piece if row is None else jnp.where(lane >= to, piece, row)
+        for layer in range(N_LAYER):
+            out_ref[pl.ds(5 * layer + k, N_TILE, stride=5 * N_LAYER), :] = row
+
+
+def unpack_kernel(z_ref, vel_ref, grad_ref, rows_ref):
     lane = lane_iota()
+    for group in range(N_TILE):
+        for r in range(8):
+            k, off = divmod(3 * CHUNK * r, 128)
+            piece = lanes_left(z_ref[pl.ds(40 * group + k, 8, stride=5), :], off)
+            if off + 3 * CHUNK > 128:
+                more = lanes_left(z_ref[pl.ds(40 * group + k + 1, 8, stride=5), :], off)
+                piece = jnp.where(lane < 128 - off, piece, more)
+            rows_ref[pl.ds(64 * group + r, 8, stride=8), :] = piece
     for f in range(3):
         for j in range(TILES):
             tile = None
             for chunk in range(128 * j // CHUNK, (128 * j + 127) // CHUNK + 1):
                 layer, t = divmod(chunk, N_TILE)
                 to = CHUNK * chunk - 128 * j
-                piece = lanes_left(z_ref[t, layer], CHUNK * f - to)
+                src = 8 * (t * N_LAYER + layer)
+                piece = lanes_left(rows_ref[src : src + 8, :], CHUNK * f - to)
                 tile = piece if tile is None else jnp.where(lane >= to, piece, tile)
             if f < 2:
                 vel_ref[f, :, 128 * j : 128 * j + 128] = tile
@@ -379,6 +401,13 @@
 
 def exchange(x, axis):
     return lax.all_to_all(x, axis, split_axis=0, concat_axis=0, tiled=True)
+
+
+def to_layers(blocks):
+    out = [blocks[0]]
+    for d in range(1, N_LAYER):
+        out.append(lax.ppermute(blocks[d], "layer", [(i, (i + d) % N_LAYER) for i in range(N_LAYER)]))
+    return out
 
 
 def on_device(
@@ -394,27 +423,28 @@
     )
     arrived = exchange(packed.reshape(N_TILE, PACK_ROWS, 128), "tile").reshape(N_TILE * PACK_ROWS, 128)
     (stiff,) = call(stiffness_kernel, [(8, COLS)], in_specs=[VMEM] * 2)(hardness, thickness)
-    (parts,) = call(
+    parts = call(
         scatter_kernel,
-        [(N_LAYER, 16, 8, 128)],
+        [(16, 8, 128)] * N_LAYER,
         scratch=[
             pltpu.VMEM((3 * PIECES * 96, DEPTH), jnp.bfloat16),
             pltpu.VMEM((256, DEPTH), jnp.bfloat16),
             pltpu.VMEM((3 * PIECES * 96, 256), F32),
+            pltpu.VMEM((4, TILES + 2, 8, 128), F32),
         ],
-        in_specs=[VMEM] * 2,
+        in_specs=[SMEM] + [VMEM] * 2,
         flops=3600000000,
         limit=16,
-    )(arrived, stiff)
-    parts = exchange(parts, "layer")
+    )(me, arrived, stiff)
+    parts = to_layers(parts)
     (blocks,) = call(
         prepare_kernel, [(7, WB, 8, 128)], scratch=[pltpu.VMEM((6, WIDE, 128), F32)], in_specs=[VMEM]
     )(arrived)
-    (chunks,) = call(chunks_kernel, [(N_TILE, 5, 8, 128)], in_specs=[VMEM])(parts)
+    (chunks,) = call(chunks_kernel, [(N_TILE, 4, 8, 128)], in_specs=[VMEM] * N_LAYER)(*parts)
     chunks = exchange(chunks, "tile")
     (shares,) = call(
         solve_kernel,
-        [(N_TILE, N_LAYER, 8, 128)],
+        [(N_TILE * N_LAYER * 5, 128)],
         scratch=[
             pltpu.VMEM((3, WIDE, 128), F32),
             pltpu.VMEM((WB, 8, 128), F32),
@@ -433,10 +463,13 @@
         flops=3600000000,
         limit=16,
     )(chunks, blocks)
-    shares = exchange(shares.reshape(N_TILE * N_LAYER, 8, 128), ("tile", "layer"))
-    velocity, gradient = call(unpack_kernel, [(2, 8, COLS), (8, COLS)], in_specs=[VMEM])(
-        shares.reshape(N_TILE, N_LAYER, 8, 128)
-    )
+    shares = exchange(shares.reshape(N_TILE * N_LAYER * 5 * 128), ("tile", "layer"))
+    velocity, gradient = call(
+        unpack_kernel,
+        [(2, 8, COLS), (8, COLS)],
+        scratch=[pltpu.VMEM((N_TILE * N_LAYER * 8, 128), F32)],
+        in_specs=[VMEM],
+    )(shares.reshape(N_TILE * N_LAYER * 5, 128))
     return velocity, gradient
 
 

time: 91.9 us -> 89.4 us (0.973)
  blocking collectives: 35.5 us -> 18.1 us
  starting transfers between devices: 12.3 us -> 23.3 us
  waiting for transfers between devices: 19.4 us -> 22.5 us
    all_to_all x2 -> x1, blocking collectives: 35.5 us -> 18.1 us  [exchange(): return lax.all_to_all(x, axis, split_axis=0, concat_axis=0, tiled=True)]
    ppermute x0 -> x7, starting transfers between devices: none -> 11.1 us  [to_layers(): lax.ppermute(blocks[d], 'layer', [(i, (i + d) % N_LAYER) for i in range(N...]
    ppermute x0 -> x7, waiting for transfers between devices: none -> 2.86 us  [to_layers(): lax.ppermute(blocks[d], 'layer', [(i, (i + d) % N_LAYER) for i in range(N...]
  transfers between devices with their start and end apart: 2 -> 9, of which waited for: 2 -> 6; matrix products, arithmetic and copies ran while one was open for 0% -> 0% of each run, Pallas kernels for 0% -> 0%
where the time goes in v3:
time: 89.4 us; the launch traced here: 89 us
  Pallas kernels  24.3 us (27%)
  starting transfers between devices  23.3 us (26%)
  waiting for transfers between devices  22.5 us (25%)
  blocking collectives  18.1 us (20%)
    all_to_all x2, waiting for transfers between devices, exchange(): return lax.all_to_all(x, axis, split_axis=0, concat_axis=0, tiled=True)  19.6 us
    all_to_all x1, blocking collectives, exchange(): return lax.all_to_all(x, axis, split_axis=0, concat_axis=0, tiled=True)  18.1 us
    pallas_call x1, Pallas kernels, on_device(): call(solve_kernel, [(N_TILE * N_LAYER * 5, 128)], scratch=[pltpu.VMEM((3,...  12.9 us
    all_to_all x2, starting transfers between devices, exchange(): return lax.all_to_all(x, axis, split_axis=0, concat_axis=0, tiled=True)  12.3 us
    ppermute x7, starting transfers between devices, to_layers(): lax.ppermute(blocks[d], 'layer', [(i, (i + d) % N_LAYER) for i in range(N...  11.1 us
    pallas_call x1, Pallas kernels, on_device(): call(scatter_kernel, [(16, 8, 128)] * N_LAYER, scratch=[pltpu.VMEM((3 * P...  5.22 us
    pallas_call x1, Pallas kernels, on_device(): call(pack_kernel, [(N_TILE * PACK_ROWS, 128)], in_specs=[SMEM] * 2 + [VME...  3.11 us
    ppermute x7, waiting for transfers between devices, to_layers(): lax.ppermute(blocks[d], 'layer', [(i, (i + d) % N_LAYER) for i in range(N...  2.86 us
  transfers between devices with their start and end apart: 9, of which 6 were waited for; matrix products, arithmetic and copies ran while one was open for 0% of the time, Pallas kernels for 0%

profile of v3, /device:TPU:1, one launch (start us, length us, event | category | flops | bytes accessed | tf_op | source)
XLA Modules:
  0.0 89.0 jit_solution(2960228574089564294)
XLA Ops:
  0.6 3.1 %shard_map.131 = f32[1408,128]{1,0:T(8,128)} custom-call(s32[1]{0:T(128)} %bitcast.me_ref, s32[1,16]{1,0:T(1,128)} %bitcast.19, s32[16,512]{1,0:T(8,128)} %bitcast.15, f32[16,512]{1,0:T(8,128)} %bitcast.16, f32[16,512]{1,0:T(8,128)} %bitcast.17, f32[16,512]{1,0:T(8,128)} %bitcast.18, f32[2,8,3072]{2,1,0:T(8,128)} %guess_ref.1, f32[8,3072]{1,0:T(8,128)} %fric_ref.1, ...), custom_call_target="tpu_custom_call" | custom-call | flops 1000000 | bytes 1000000 | tf_op jit(solution)/shard_map/pallas_call | solution.py:419
  3.7 0.0 copy-start
  3.7 0.0 copy-start.1
  3.8 8.7 %all-to-all-start = ((f32[16,88,128]{2,1,0:T(8,128)}), f32[16,88,128]{2,1,0:T(8,128)S(1)}, u32[]{:S(2)}, u32[]{:S(2)}) async-start(f32[16,88,128]{2,1,0:T(8,128)} %bitcast.14), calls=%async_computation | async-start | bytes 1441792 | tf_op jit(solution)/shard_map/all_to_all | solution.py:403
  12.5 0.0 copy-done
  12.5 0.0 copy-done.1
  12.5 12.1 %all-to-all-done = f32[16,88,128]{2,1,0:T(8,128)S(1)} async-done(((f32[16,88,128]{2,1,0:T(8,128)}), f32[16,88,128]{2,1,0:T(8,128)S(1)}, u32[]{:S(2)}, u32[]{:S(2)}) %all-to-all-start) | async-done | bytes 720928 | tf_op jit(solution)/shard_map/all_to_all | solution.py:403
  24.7 5.2 %shard_map.133 = (f32[16,8,128]{2,1,0:T(8,128)S(1)}, f32[16,8,128]{2,1,0:T(8,128)S(1)}, f32[16,8,128]{2,1,0:T(8,128)S(1)}, f32[16,8,128]{2,1,0:T(8,128)S(1)}, f3...) custom-call(s32[1]{0:T(128)} %bitcast.me_ref, ...), custom_call_target="tpu_custom_call" | custom-call | flops 3600000000 | bytes 1000000 | tf_op jit(solution)/shard_map/pallas_call | solution.py:426
  29.9 3.5 %collective-permute-start = (f32[16,8,128]{2,1,0:T(8,128)S(1)}, f32[16,8,128]{2,1,0:T(8,128)S(1)}, u32[]{:S(2)}, u32[]{:S(2)}) collective-permute-start(f32[16,8,128]{2,1,0:T(8,128)S(1)} %get-tuple-element.11), channel_id=1, source_target_pairs={{0,1},{1,2},{2,3},{3,4},{4,5},{5,6},{6,7},{7,0},{8,9},{9,10},{10,1... | collective-permute-start | bytes 196616 | tf_op jit(solution)/shard_map/ppermute | solution.py:409
  33.4 1.2 %collective-permute-start.1 = (f32[16,8,128]{2,1,0:T(8,128)S(1)}, f32[16,8,128]{2,1,0:T(8,128)S(1)}, u32[]{:S(2)}, u32[]{:S(2)}) collective-permute-start(f32[16,8,128]{2,1,0:T(8,128)S(1)} %get-tuple-element.12), channel_id=1, source_target_pairs={{0,2},{1,3},{2,4},{3,5},{4,6},{5,7},{6,0},{7,1},{8,10},{9,11},{10,... | collective-permute-start | bytes 196616 | tf_op jit(solution)/shard_map/ppermute | solution.py:409
  34.6 1.6 %collective-permute-start.2 = (f32[16,8,128]{2,1,0:T(8,128)S(1)}, f32[16,8,128]{2,1,0:T(8,128)S(1)}, u32[]{:S(2)}, u32[]{:S(2)}) collective-permute-start(f32[16,8,128]{2,1,0:T(8,128)S(1)} %get-tuple-element.13), channel_id=1, source_target_pairs={{0,3},{1,4},{2,5},{3,6},{4,7},{5,0},{6,1},{7,2},{8,11},{9,12},{10,... | collective-permute-start | bytes 196616 | tf_op jit(solution)/shard_map/ppermute | solution.py:409
  36.2 0.5 collective-permute-start.3
  36.7 1.9 %collective-permute-start.4 = (f32[16,8,128]{2,1,0:T(8,128)S(1)}, f32[16,8,128]{2,1,0:T(8,128)S(1)}, u32[]{:S(2)}, u32[]{:S(2)}) collective-permute-start(f32[16,8,128]{2,1,0:T(8,128)S(1)} %get-tuple-element.15), channel_id=1, source_target_pairs={{0,5},{1,6},{2,7},{3,0},{4,1},{5,2},{6,3},{7,4},{8,13},{9,14},{10,... | collective-permute-start | bytes 196616 | tf_op jit(solution)/shard_map/ppermute | solution.py:409
  38.7 0.0 collective-permute-done.refs_1_
  38.7 0.7 collective-permute-start.5
  39.3 0.0 collective-permute-done.1.refs_2_
  39.3 1.7 %collective-permute-start.6 = (f32[16,8,128]{2,1,0:T(8,128)S(1)}, f32[16,8,128]{2,1,0:T(8,128)S(1)}, u32[]{:S(2)}, u32[]{:S(2)}) collective-permute-start(f32[16,8,128]{2,1,0:T(8,128)S(1)} %get-tuple-element.17), channel_id=1, source_target_pairs={{0,7},{1,0},{2,1},{3,2},{4,3},{5,4},{6,5},{7,6},{8,15},{9,8},{10,9... | collective-permute-start | bytes 196616 | tf_op jit(solution)/shard_map/ppermute | solution.py:409
  41.0 0.0 collective-permute-done.2.refs_3_
  41.0 0.9 %collective-permute-done.3.refs_4_ = f32[16,8,128]{2,1,0:T(8,128)S(1)} collective-permute-done((f32[16,8,128]{2,1,0:T(8,128)S(1)}, f32[16,8,128]{2,1,0:T(8,128)S(1)}, u32[]{:S(2)}, u32[]{:S(2)}) %collective-permute-start.3) | collective-permute-done | bytes 65568 | tf_op jit(solution)/shard_map/ppermute | solution.py:409
  41.9 0.5 collective-permute-done.4.refs_5_
  42.4 0.1 collective-permute-done.5.refs_6_
  42.5 1.4 %collective-permute-done.6.refs_7_ = f32[16,8,128]{2,1,0:T(8,128)S(1)} collective-permute-done((f32[16,8,128]{2,1,0:T(8,128)S(1)}, f32[16,8,128]{2,1,0:T(8,128)S(1)}, u32[]{:S(2)}, u32[]{:S(2)}) %collective-permute-start.6) | collective-permute-done | bytes 65568 | tf_op jit(solution)/shard_map/ppermute | solution.py:409
  43.9 1.3 %shard_map.134 = f32[16,4,8,128]{3,2,1,0:T(8,128)} custom-call(f32[16,8,128]{2,1,0:T(8,128)S(1)} %get-tuple-element.10.refs_0_, f32[16,8,128]{2,1,0:T(8,128)S(1)} %collective-permute-done.refs_1_, f32[16,8,128]{2,1,0:T(8,128)S(1)} %collective-permute-done.1.refs_2_, f32[16,8,128]{2,1,0:T(8,128)S(1)} %collective-permute-done.2.refs_3_, ...), custom_call_target="tpu_custom_call" | custom-call | flops 1000000 | bytes 1000000 | tf_op jit(solution)/shard_map/pallas_call | solution.py:443
  45.1 3.5 %all-to-all-start.1 = ((f32[16,4,8,128]{3,2,1,0:T(8,128)}), f32[16,4,8,128]{3,2,1,0:T(8,128)S(1)}, u32[]{:S(2)}, u32[]{:S(2)}) async-start(f32[16,4,8,128]{3,2,1,0:T(8,128)} %shard_map.134), calls=%async_computation.1 | async-start | bytes 524288 | tf_op jit(solution)/shard_map/all_to_all | solution.py:403
  48.7 0.4 shard_map.135.blk
  49.1 7.5 %all-to-all-done.1.z_ref = f32[16,4,8,128]{3,2,1,0:T(8,128)S(1)} async-done(((f32[16,4,8,128]{3,2,1,0:T(8,128)}), f32[16,4,8,128]{3,2,1,0:T(8,128)S(1)}, u32[]{:S(2)}, u32[]{:S(2)}) %all-to-all-start.1) | async-done | bytes 262176 | tf_op jit(solution)/shard_map/all_to_all | solution.py:403
  56.6 12.9 %shard_map.136 = f32[640,128]{1,0:T(8,128)S(1)} custom-call(f32[16,4,8,128]{3,2,1,0:T(8,128)S(1)} %all-to-all-done.1.z_ref, f32[7,23,8,128]{3,2,1,0:T(8,128)S(1)} %shard_map.135.blk), custom_call_target="tpu_custom_call" | custom-call | flops 3600000000 | bytes 1000000 | tf_op jit(solution)/shard_map/pallas_call | solution.py:445
  69.5 18.1 %all_to_all.19 = f32[128,640,1]{1,2,0:T(1,128)S(1)} all-to-all(f32[128,640,1]{1,2,0:T(1,128)S(1)} %bitcast.13), channel_id=1, replica_groups=mesh['tile'=16,'layer'=8] {'tile','layer'}, dimensions={0} | all-to-all | bytes 655360 | tf_op jit(solution)/shard_map/all_to_all | solution.py:403
  87.6 1.4 %shard_map.137 = (f32[2,8,3072]{2,1,0:T(8,128)}, f32[8,3072]{1,0:T(8,128)}) custom-call(f32[640,128]{1,0:T(8,128)S(1)} %bitcast.12), custom_call_target="tpu_custom_call" | custom-call | flops 1000000 | bytes 1000000 | tf_op jit(solution)/shard_map/pallas_call | solution.py:467
  (1 shorter events, 0.0 us)
Async XLA Ops:
  3.7 8.7 %copy-start = (f32[4,8,3072]{2,1,0:T(8,128)S(1)}, f32[4,8,3072]{2,1,0:T(8,128)}, u32[]{:S(2)}) copy-start(f32[4,8,3072]{2,1,0:T(8,128)} %hard_ref.1) | copy-start | bytes 1179652
  3.7 8.8 %copy-start.1 = (f32[8,3072]{1,0:T(8,128)S(1)}, f32[8,3072]{1,0:T(8,128)}, u32[]{:S(2)}) copy-start(f32[8,3072]{1,0:T(8,128)} %thick_ref.1) | copy-start | bytes 294916
  3.8 20.9 %all-to-all-start = ((f32[16,88,128]{2,1,0:T(8,128)}), f32[16,88,128]{2,1,0:T(8,128)S(1)}, u32[]{:S(2)}, u32[]{:S(2)}) async-start(f32[16,88,128]{2,1,0:T(8,128)} %bitcast.14), calls=%async_computation | async-start | bytes 1441792 | tf_op jit(solution)/shard_map/all_to_all | solution.py:403
  29.9 8.8 %collective-permute-start = (f32[16,8,128]{2,1,0:T(8,128)S(1)}, f32[16,8,128]{2,1,0:T(8,128)S(1)}, u32[]{:S(2)}, u32[]{:S(2)}) collective-permute-start(f32[16,8,128]{2,1,0:T(8,128)S(1)} %get-tuple-element.11), channel_id=1, source_target_pairs={{0,1},{1,2},{2,3},{3,4},{4,5},{5,6},{6,7},{7,0},{8,9},{9,10},{10,1... | collective-permute-start | bytes 196616 | tf_op jit(solution)/shard_map/ppermute | solution.py:409
  33.4 6.0 %collective-permute-start.1 = (f32[16,8,128]{2,1,0:T(8,128)S(1)}, f32[16,8,128]{2,1,0:T(8,128)S(1)}, u32[]{:S(2)}, u32[]{:S(2)}) collective-permute-start(f32[16,8,128]{2,1,0:T(8,128)S(1)} %get-tuple-element.12), channel_id=1, source_target_pairs={{0,2},{1,3},{2,4},{3,5},{4,6},{5,7},{6,0},{7,1},{8,10},{9,11},{10,... | collective-permute-start | bytes 196616 | tf_op jit(solution)/shard_map/ppermute | solution.py:409
  34.6 6.4 %collective-permute-start.2 = (f32[16,8,128]{2,1,0:T(8,128)S(1)}, f32[16,8,128]{2,1,0:T(8,128)S(1)}, u32[]{:S(2)}, u32[]{:S(2)}) collective-permute-start(f32[16,8,128]{2,1,0:T(8,128)S(1)} %get-tuple-element.13), channel_id=1, source_target_pairs={{0,3},{1,4},{2,5},{3,6},{4,7},{5,0},{6,1},{7,2},{8,11},{9,12},{10,... | collective-permute-start | bytes 196616 | tf_op jit(solution)/shard_map/ppermute | solution.py:409
  36.2 5.7 %collective-permute-start.3 = (f32[16,8,128]{2,1,0:T(8,128)S(1)}, f32[16,8,128]{2,1,0:T(8,128)S(1)}, u32[]{:S(2)}, u32[]{:S(2)}) collective-permute-start(f32[16,8,128]{2,1,0:T(8,128)S(1)} %get-tuple-element.14), channel_id=1, source_target_pairs={{0,4},{1,5},{2,6},{3,7},{4,0},{5,1},{6,2},{7,3},{8,12},{9,13},{10,... | collective-permute-start | bytes 196616 | tf_op jit(solution)/shard_map/ppermute | solution.py:409
  36.7 5.7 %collective-permute-start.4 = (f32[16,8,128]{2,1,0:T(8,128)S(1)}, f32[16,8,128]{2,1,0:T(8,128)S(1)}, u32[]{:S(2)}, u32[]{:S(2)}) collective-permute-start(f32[16,8,128]{2,1,0:T(8,128)S(1)} %get-tuple-element.15), channel_id=1, source_target_pairs={{0,5},{1,6},{2,7},{3,0},{4,1},{5,2},{6,3},{7,4},{8,13},{9,14},{10,... | collective-permute-start | bytes 196616 | tf_op jit(solution)/shard_map/ppermute | solution.py:409
  38.7 3.8 %collective-permute-start.5 = (f32[16,8,128]{2,1,0:T(8,128)S(1)}, f32[16,8,128]{2,1,0:T(8,128)S(1)}, u32[]{:S(2)}, u32[]{:S(2)}) collective-permute-start(f32[16,8,128]{2,1,0:T(8,128)S(1)} %get-tuple-element.16), channel_id=1, source_target_pairs={{0,6},{1,7},{2,0},{3,1},{4,2},{5,3},{6,4},{7,5},{8,14},{9,15},{10,... | collective-permute-start | bytes 196616 | tf_op jit(solution)/shard_map/ppermute | solution.py:409
  39.3 4.5 %collective-permute-start.6 = (f32[16,8,128]{2,1,0:T(8,128)S(1)}, f32[16,8,128]{2,1,0:T(8,128)S(1)}, u32[]{:S(2)}, u32[]{:S(2)}) collective-permute-start(f32[16,8,128]{2,1,0:T(8,128)S(1)} %get-tuple-element.17), channel_id=1, source_target_pairs={{0,7},{1,0},{2,1},{3,2},{4,3},{5,4},{6,5},{7,6},{8,15},{9,8},{10,9... | collective-permute-start | bytes 196616 | tf_op jit(solution)/shard_map/ppermute | solution.py:409
  45.1 11.5 %all-to-all-start.1 = ((f32[16,4,8,128]{3,2,1,0:T(8,128)}), f32[16,4,8,128]{3,2,1,0:T(8,128)S(1)}, u32[]{:S(2)}, u32[]{:S(2)}) async-start(f32[16,4,8,128]{3,2,1,0:T(8,128)} %shard_map.134), calls=%async_computation.1 | async-start | bytes 524288 | tf_op jit(solution)/shard_map/all_to_all | solution.py:403

commit v4 on v3

--- a/solution.py
+++ b/solution.py
@@ -24,6 +24,7 @@
 F32 = jnp.float32
 PACK_ROWS = 8 * 11
 PIECES = 3
+UNROLL = 20
 DEPTH = 2048
 OBS_ROWS = PACK_ROWS
 OBS_AT = 72
@@ -218,11 +219,12 @@
 
 def sweeps(coef_ref, gu_ref, gv_ref, one, two, n):
     def body(_, carry):
-        sweep(coef_ref, gu_ref, gv_ref, one, two, n, 0)
-        sweep(coef_ref, gu_ref, gv_ref, two, one, n, n // 2)
+        for k in range(UNROLL):
+            old, new = (one, two) if k % 2 == 0 else (two, one)
+            sweep(coef_ref, gu_ref, gv_ref, old, new, n, (n // 4 * k) % n)
         return carry
 
-    lax.fori_loop(0, SWEEPS // 2, body, 0)
+    lax.fori_loop(0, SWEEPS // UNROLL, body, 0)
 
 
 def up_down():

time: 89.4 us -> 86.1 us (0.963)
  Pallas kernels: 24.3 us -> 21.1 us
    pallas_call x1, Pallas kernels: 12.9 us -> 9.66 us  [on_device(): call(solve_kernel, [(N_TILE * N_LAYER * 5, 128)], scratch=[pltpu.VMEM((3,...]
  transfers between devices with their start and end apart: 9 -> 9, of which waited for: 6 -> 6; matrix products, arithmetic and copies ran while one was open for 0% -> 0% of each run, Pallas kernels for 0% -> 1%
where the time goes in v4:
time: 86.1 us; the launch traced here: 85.8 us
  starting transfers between devices  23.3 us (27%)
  waiting for transfers between devices  22.5 us (26%)
  Pallas kernels  21.1 us (25%)
  blocking collectives  18.1 us (21%)
    all_to_all x2, waiting for transfers between devices, exchange(): return lax.all_to_all(x, axis, split_axis=0, concat_axis=0, tiled=True)  19.6 us
    all_to_all x1, blocking collectives, exchange(): return lax.all_to_all(x, axis, split_axis=0, concat_axis=0, tiled=True)  18.1 us
    all_to_all x2, starting transfers between devices, exchange(): return lax.all_to_all(x, axis, split_axis=0, concat_axis=0, tiled=True)  12.3 us
    ppermute x7, starting transfers between devices, to_layers(): lax.ppermute(blocks[d], 'layer', [(i, (i + d) % N_LAYER) for i in range(N...  11.1 us
    pallas_call x1, Pallas kernels, on_device(): call(solve_kernel, [(N_TILE * N_LAYER * 5, 128)], scratch=[pltpu.VMEM((3,...  9.66 us
    pallas_call x1, Pallas kernels, on_device(): call(scatter_kernel, [(16, 8, 128)] * N_LAYER, scratch=[pltpu.VMEM((3 * P...  5.22 us
    pallas_call x1, Pallas kernels, on_device(): call(pack_kernel, [(N_TILE * PACK_ROWS, 128)], in_specs=[SMEM] * 2 + [VME...  3.11 us
    ppermute x7, waiting for transfers between devices, to_layers(): lax.ppermute(blocks[d], 'layer', [(i, (i + d) % N_LAYER) for i in range(N...  2.86 us
  transfers between devices with their start and end apart: 9, of which 6 were waited for; matrix products, arithmetic and copies ran while one was open for 0% of the time, Pallas kernels for 1%

profile of v4, /device:TPU:1, one launch (start us, length us, event | category | flops | bytes accessed | tf_op | source)
XLA Modules:
  0.0 85.8 jit_solution(9525957768513334588)
XLA Ops:
  0.6 3.1 %shard_map.131 = f32[1408,128]{1,0:T(8,128)} custom-call(s32[1]{0:T(128)} %bitcast.me_ref, s32[1,16]{1,0:T(1,128)} %bitcast.19, s32[16,512]{1,0:T(8,128)} %bitcast.15, f32[16,512]{1,0:T(8,128)} %bitcast.16, f32[16,512]{1,0:T(8,128)} %bitcast.17, f32[16,512]{1,0:T(8,128)} %bitcast.18, f32[2,8,3072]{2,1,0:T(8,128)} %guess_ref.1, f32[8,3072]{1,0:T(8,128)} %fric_ref.1, ...), custom_call_target="tpu_custom_call" | custom-call | flops 1000000 | bytes 1000000 | tf_op jit(solution)/shard_map/pallas_call | solution.py:421
  3.7 0.0 copy-start
  3.7 0.0 copy-start.1
  3.8 8.7 %all-to-all-start = ((f32[16,88,128]{2,1,0:T(8,128)}), f32[16,88,128]{2,1,0:T(8,128)S(1)}, u32[]{:S(2)}, u32[]{:S(2)}) async-start(f32[16,88,128]{2,1,0:T(8,128)} %bitcast.14), calls=%async_computation | async-start | bytes 1441792 | tf_op jit(solution)/shard_map/all_to_all | solution.py:405
  12.5 0.0 copy-done
  12.5 0.0 copy-done.1
  12.5 12.1 %all-to-all-done = f32[16,88,128]{2,1,0:T(8,128)S(1)} async-done(((f32[16,88,128]{2,1,0:T(8,128)}), f32[16,88,128]{2,1,0:T(8,128)S(1)}, u32[]{:S(2)}, u32[]{:S(2)}) %all-to-all-start) | async-done | bytes 720928 | tf_op jit(solution)/shard_map/all_to_all | solution.py:405
  24.7 5.2 %shard_map.133 = (f32[16,8,128]{2,1,0:T(8,128)S(1)}, f32[16,8,128]{2,1,0:T(8,128)S(1)}, f32[16,8,128]{2,1,0:T(8,128)S(1)}, f32[16,8,128]{2,1,0:T(8,128)S(1)}, f3...) custom-call(s32[1]{0:T(128)} %bitcast.me_ref, ...), custom_call_target="tpu_custom_call" | custom-call | flops 3600000000 | bytes 1000000 | tf_op jit(solution)/shard_map/pallas_call | solution.py:428
  29.9 3.5 %collective-permute-start = (f32[16,8,128]{2,1,0:T(8,128)S(1)}, f32[16,8,128]{2,1,0:T(8,128)S(1)}, u32[]{:S(2)}, u32[]{:S(2)}) collective-permute-start(f32[16,8,128]{2,1,0:T(8,128)S(1)} %get-tuple-element.11), channel_id=1, source_target_pairs={{0,1},{1,2},{2,3},{3,4},{4,5},{5,6},{6,7},{7,0},{8,9},{9,10},{10,1... | collective-permute-start | bytes 196616 | tf_op jit(solution)/shard_map/ppermute | solution.py:411
  33.4 1.2 %collective-permute-start.1 = (f32[16,8,128]{2,1,0:T(8,128)S(1)}, f32[16,8,128]{2,1,0:T(8,128)S(1)}, u32[]{:S(2)}, u32[]{:S(2)}) collective-permute-start(f32[16,8,128]{2,1,0:T(8,128)S(1)} %get-tuple-element.12), channel_id=1, source_target_pairs={{0,2},{1,3},{2,4},{3,5},{4,6},{5,7},{6,0},{7,1},{8,10},{9,11},{10,... | collective-permute-start | bytes 196616 | tf_op jit(solution)/shard_map/ppermute | solution.py:411
  34.6 1.6 %collective-permute-start.2 = (f32[16,8,128]{2,1,0:T(8,128)S(1)}, f32[16,8,128]{2,1,0:T(8,128)S(1)}, u32[]{:S(2)}, u32[]{:S(2)}) collective-permute-start(f32[16,8,128]{2,1,0:T(8,128)S(1)} %get-tuple-element.13), channel_id=1, source_target_pairs={{0,3},{1,4},{2,5},{3,6},{4,7},{5,0},{6,1},{7,2},{8,11},{9,12},{10,... | collective-permute-start | bytes 196616 | tf_op jit(solution)/shard_map/ppermute | solution.py:411
  36.2 0.5 collective-permute-start.3
  36.7 1.9 %collective-permute-start.4 = (f32[16,8,128]{2,1,0:T(8,128)S(1)}, f32[16,8,128]{2,1,0:T(8,128)S(1)}, u32[]{:S(2)}, u32[]{:S(2)}) collective-permute-start(f32[16,8,128]{2,1,0:T(8,128)S(1)} %get-tuple-element.15), channel_id=1, source_target_pairs={{0,5},{1,6},{2,7},{3,0},{4,1},{5,2},{6,3},{7,4},{8,13},{9,14},{10,... | collective-permute-start | bytes 196616 | tf_op jit(solution)/shard_map/ppermute | solution.py:411
  38.7 0.0 collective-permute-done.refs_1_
  38.7 0.7 collective-permute-start.5
  39.3 0.0 collective-permute-done.1.refs_2_
  39.3 1.7 %collective-permute-start.6 = (f32[16,8,128]{2,1,0:T(8,128)S(1)}, f32[16,8,128]{2,1,0:T(8,128)S(1)}, u32[]{:S(2)}, u32[]{:S(2)}) collective-permute-start(f32[16,8,128]{2,1,0:T(8,128)S(1)} %get-tuple-element.17), channel_id=1, source_target_pairs={{0,7},{1,0},{2,1},{3,2},{4,3},{5,4},{6,5},{7,6},{8,15},{9,8},{10,9... | collective-permute-start | bytes 196616 | tf_op jit(solution)/shard_map/ppermute | solution.py:411
  41.0 0.0 collective-permute-done.2.refs_3_
  41.0 0.9 %collective-permute-done.3.refs_4_ = f32[16,8,128]{2,1,0:T(8,128)S(1)} collective-permute-done((f32[16,8,128]{2,1,0:T(8,128)S(1)}, f32[16,8,128]{2,1,0:T(8,128)S(1)}, u32[]{:S(2)}, u32[]{:S(2)}) %collective-permute-start.3) | collective-permute-done | bytes 65568 | tf_op jit(solution)/shard_map/ppermute | solution.py:411
  41.9 0.5 collective-permute-done.4.refs_5_
  42.4 0.1 collective-permute-done.5.refs_6_
  42.5 1.4 %collective-permute-done.6.refs_7_ = f32[16,8,128]{2,1,0:T(8,128)S(1)} collective-permute-done((f32[16,8,128]{2,1,0:T(8,128)S(1)}, f32[16,8,128]{2,1,0:T(8,128)S(1)}, u32[]{:S(2)}, u32[]{:S(2)}) %collective-permute-start.6) | collective-permute-done | bytes 65568 | tf_op jit(solution)/shard_map/ppermute | solution.py:411
  43.9 1.3 %shard_map.134 = f32[16,4,8,128]{3,2,1,0:T(8,128)} custom-call(f32[16,8,128]{2,1,0:T(8,128)S(1)} %get-tuple-element.10.refs_0_, f32[16,8,128]{2,1,0:T(8,128)S(1)} %collective-permute-done.refs_1_, f32[16,8,128]{2,1,0:T(8,128)S(1)} %collective-permute-done.1.refs_2_, f32[16,8,128]{2,1,0:T(8,128)S(1)} %collective-permute-done.2.refs_3_, ...), custom_call_target="tpu_custom_call" | custom-call | flops 1000000 | bytes 1000000 | tf_op jit(solution)/shard_map/pallas_call | solution.py:445
  45.1 3.5 %all-to-all-start.1 = ((f32[16,4,8,128]{3,2,1,0:T(8,128)}), f32[16,4,8,128]{3,2,1,0:T(8,128)S(1)}, u32[]{:S(2)}, u32[]{:S(2)}) async-start(f32[16,4,8,128]{3,2,1,0:T(8,128)} %shard_map.134), calls=%async_computation.1 | async-start | bytes 524288 | tf_op jit(solution)/shard_map/all_to_all | solution.py:405
  48.7 0.4 shard_map.135.blk
  49.1 7.5 %all-to-all-done.1.z_ref = f32[16,4,8,128]{3,2,1,0:T(8,128)S(1)} async-done(((f32[16,4,8,128]{3,2,1,0:T(8,128)}), f32[16,4,8,128]{3,2,1,0:T(8,128)S(1)}, u32[]{:S(2)}, u32[]{:S(2)}) %all-to-all-start.1) | async-done | bytes 262176 | tf_op jit(solution)/shard_map/all_to_all | solution.py:405
  56.6 9.7 %shard_map.136 = f32[640,128]{1,0:T(8,128)S(1)} custom-call(f32[16,4,8,128]{3,2,1,0:T(8,128)S(1)} %all-to-all-done.1.z_ref, f32[7,23,8,128]{3,2,1,0:T(8,128)S(1)} %shard_map.135.blk), custom_call_target="tpu_custom_call" | custom-call | flops 3600000000 | bytes 1000000 | tf_op jit(solution)/shard_map/pallas_call | solution.py:447
  66.3 18.1 %all_to_all.19 = f32[128,640,1]{1,2,0:T(1,128)S(1)} all-to-all(f32[128,640,1]{1,2,0:T(1,128)S(1)} %bitcast.13), channel_id=1, replica_groups=mesh['tile'=16,'layer'=8] {'tile','layer'}, dimensions={0} | all-to-all | bytes 655360 | tf_op jit(solution)/shard_map/all_to_all | solution.py:405
  84.4 1.4 %shard_map.137 = (f32[2,8,3072]{2,1,0:T(8,128)}, f32[8,3072]{1,0:T(8,128)}) custom-call(f32[640,128]{1,0:T(8,128)S(1)} %bitcast.12), custom_call_target="tpu_custom_call" | custom-call | flops 1000000 | bytes 1000000 | tf_op jit(solution)/shard_map/pallas_call | solution.py:469
  (1 shorter events, 0.0 us)
Async XLA Ops:
  3.7 8.7 %copy-start = (f32[4,8,3072]{2,1,0:T(8,128)S(1)}, f32[4,8,3072]{2,1,0:T(8,128)}, u32[]{:S(2)}) copy-start(f32[4,8,3072]{2,1,0:T(8,128)} %hard_ref.1) | copy-start | bytes 1179652
  3.7 8.8 %copy-start.1 = (f32[8,3072]{1,0:T(8,128)S(1)}, f32[8,3072]{1,0:T(8,128)}, u32[]{:S(2)}) copy-start(f32[8,3072]{1,0:T(8,128)} %thick_ref.1) | copy-start | bytes 294916
  3.8 20.9 %all-to-all-start = ((f32[16,88,128]{2,1,0:T(8,128)}), f32[16,88,128]{2,1,0:T(8,128)S(1)}, u32[]{:S(2)}, u32[]{:S(2)}) async-start(f32[16,88,128]{2,1,0:T(8,128)} %bitcast.14), calls=%async_computation | async-start | bytes 1441792 | tf_op jit(solution)/shard_map/all_to_all | solution.py:405
  29.9 8.8 %collective-permute-start = (f32[16,8,128]{2,1,0:T(8,128)S(1)}, f32[16,8,128]{2,1,0:T(8,128)S(1)}, u32[]{:S(2)}, u32[]{:S(2)}) collective-permute-start(f32[16,8,128]{2,1,0:T(8,128)S(1)} %get-tuple-element.11), channel_id=1, source_target_pairs={{0,1},{1,2},{2,3},{3,4},{4,5},{5,6},{6,7},{7,0},{8,9},{9,10},{10,1... | collective-permute-start | bytes 196616 | tf_op jit(solution)/shard_map/ppermute | solution.py:411
  33.4 6.0 %collective-permute-start.1 = (f32[16,8,128]{2,1,0:T(8,128)S(1)}, f32[16,8,128]{2,1,0:T(8,128)S(1)}, u32[]{:S(2)}, u32[]{:S(2)}) collective-permute-start(f32[16,8,128]{2,1,0:T(8,128)S(1)} %get-tuple-element.12), channel_id=1, source_target_pairs={{0,2},{1,3},{2,4},{3,5},{4,6},{5,7},{6,0},{7,1},{8,10},{9,11},{10,... | collective-permute-start | bytes 196616 | tf_op jit(solution)/shard_map/ppermute | solution.py:411
  34.6 6.4 %collective-permute-start.2 = (f32[16,8,128]{2,1,0:T(8,128)S(1)}, f32[16,8,128]{2,1,0:T(8,128)S(1)}, u32[]{:S(2)}, u32[]{:S(2)}) collective-permute-start(f32[16,8,128]{2,1,0:T(8,128)S(1)} %get-tuple-element.13), channel_id=1, source_target_pairs={{0,3},{1,4},{2,5},{3,6},{4,7},{5,0},{6,1},{7,2},{8,11},{9,12},{10,... | collective-permute-start | bytes 196616 | tf_op jit(solution)/shard_map/ppermute | solution.py:411
  36.2 5.7 %collective-permute-start.3 = (f32[16,8,128]{2,1,0:T(8,128)S(1)}, f32[16,8,128]{2,1,0:T(8,128)S(1)}, u32[]{:S(2)}, u32[]{:S(2)}) collective-permute-start(f32[16,8,128]{2,1,0:T(8,128)S(1)} %get-tuple-element.14), channel_id=1, source_target_pairs={{0,4},{1,5},{2,6},{3,7},{4,0},{5,1},{6,2},{7,3},{8,12},{9,13},{10,... | collective-permute-start | bytes 196616 | tf_op jit(solution)/shard_map/ppermute | solution.py:411
  36.7 5.7 %collective-permute-start.4 = (f32[16,8,128]{2,1,0:T(8,128)S(1)}, f32[16,8,128]{2,1,0:T(8,128)S(1)}, u32[]{:S(2)}, u32[]{:S(2)}) collective-permute-start(f32[16,8,128]{2,1,0:T(8,128)S(1)} %get-tuple-element.15), channel_id=1, source_target_pairs={{0,5},{1,6},{2,7},{3,0},{4,1},{5,2},{6,3},{7,4},{8,13},{9,14},{10,... | collective-permute-start | bytes 196616 | tf_op jit(solution)/shard_map/ppermute | solution.py:411
  38.7 3.8 %collective-permute-start.5 = (f32[16,8,128]{2,1,0:T(8,128)S(1)}, f32[16,8,128]{2,1,0:T(8,128)S(1)}, u32[]{:S(2)}, u32[]{:S(2)}) collective-permute-start(f32[16,8,128]{2,1,0:T(8,128)S(1)} %get-tuple-element.16), channel_id=1, source_target_pairs={{0,6},{1,7},{2,0},{3,1},{4,2},{5,3},{6,4},{7,5},{8,14},{9,15},{10,... | collective-permute-start | bytes 196616 | tf_op jit(solution)/shard_map/ppermute | solution.py:411
  39.3 4.5 %collective-permute-start.6 = (f32[16,8,128]{2,1,0:T(8,128)S(1)}, f32[16,8,128]{2,1,0:T(8,128)S(1)}, u32[]{:S(2)}, u32[]{:S(2)}) collective-permute-start(f32[16,8,128]{2,1,0:T(8,128)S(1)} %get-tuple-element.17), channel_id=1, source_target_pairs={{0,7},{1,0},{2,1},{3,2},{4,3},{5,4},{6,5},{7,6},{8,15},{9,8},{10,9... | collective-permute-start | bytes 196616 | tf_op jit(solution)/shard_map/ppermute | solution.py:411
  45.1 11.5 %all-to-all-start.1 = ((f32[16,4,8,128]{3,2,1,0:T(8,128)}), f32[16,4,8,128]{3,2,1,0:T(8,128)S(1)}, u32[]{:S(2)}, u32[]{:S(2)}) async-start(f32[16,4,8,128]{3,2,1,0:T(8,128)} %shard_map.134), calls=%async_computation.1 | async-start | bytes 524288 | tf_op jit(solution)/shard_map/all_to_all | solution.py:405

commit v5 on v4

--- a/solution.py
+++ b/solution.py
@@ -14,6 +14,7 @@
 TILES = COLS // 128
 N_TILE = 16
 N_LAYER = 8
+N_CHIP = N_LAYER // 2
 BLOCK = 512
 CHUNK = 24
 WIDE = CHUNK + 4 * SWEEPS
@@ -95,7 +96,7 @@
 
 
 def scatter_kernel(me_ref, obs_ref, stiff_ref, *refs):
-    outs, (lhs_ref, rhs_ref, acc_ref, turned_ref) = refs[:N_LAYER], refs[N_LAYER:]
+    outs, (lhs_ref, rhs_ref, acc_ref, turned_ref) = refs[:2], refs[2:]
     acc_ref[...] = jnp.zeros_like(acc_ref)
     step16 = lax.broadcasted_iota(jnp.int32, (16, 128), 0).astype(F32).astype(jnp.bfloat16)
     zero16 = jnp.zeros((16, 128), jnp.bfloat16)
@@ -146,18 +147,25 @@
             total = total + acc_ref[(PIECES * f + k) * 96 : (PIECES * f + k + 1) * 96, :]
         tiles = [total[8 * (g // 2) : 8 * (g // 2) + 8, 128 * (g % 2) : 128 * (g % 2) + 128] for g in range(TILES)]
         turn(f + 1, tiles, 88)
-    for d in range(N_LAYER):
-        first = 3 * ((me_ref[0] + d) & (N_LAYER - 1))
-        for f in range(4):
-            for k in range(4):
-                tile = turned_ref[f, first + k]
-                if f == 1 and k == 3:
-                    tile = jnp.where(lane < 80, tile, pltpu.roll(turned_ref[0, first + 4], 80, 1))
-                outs[d][4 * f + k] = tile
+    chip, core = me_ref[0] >> 1, me_ref[0] & 1
+    for side in range(2):
+        for d in range(N_CHIP):
+            first = 3 * (2 * ((chip + d) & (N_CHIP - 1)) + (core ^ side))
+            for f in range(4):
+                for k in range(4):
+                    tile = turned_ref[f, first + k]
+                    if f == 1 and k == 3:
+                        tile = jnp.where(lane < 80, tile, pltpu.roll(turned_ref[0, first + 4], 80, 1))
+                    outs[side][d, 4 * f + k] = tile
+
+
+def add_kernel(a_ref, b_ref, *outs):
+    for d in range(N_CHIP):
+        outs[d][...] = a_ref[d] + b_ref[d]
 
 
 def chunks_kernel(*refs):
-    parts, out_ref = refs[:N_LAYER], refs[N_LAYER]
+    parts, out_ref = refs[:N_CHIP], refs[N_CHIP]
     lane = lane_iota()
 
     def summed(k):
@@ -405,10 +413,13 @@
     return lax.all_to_all(x, axis, split_axis=0, concat_axis=0, tiled=True)
 
 
-def to_layers(blocks):
+def to_layers(own, other):
+    moved = lax.ppermute(other, "layer", [(i, i ^ 1) for i in range(N_LAYER)])
+    shape = own.shape[1:]
+    blocks = call(add_kernel, [shape] * N_CHIP, in_specs=[VMEM] * 2)(own, moved)
     out = [blocks[0]]
-    for d in range(1, N_LAYER):
-        out.append(lax.ppermute(blocks[d], "layer", [(i, (i + d) % N_LAYER) for i in range(N_LAYER)]))
+    for d in range(1, N_CHIP):
+        out.append(lax.ppermute(blocks[d], "layer", [(i, (i + 2 * d) % N_LAYER) for i in range(N_LAYER)]))
     return out
 
 
@@ -427,7 +438,7 @@
     (stiff,) = call(stiffness_kernel, [(8, COLS)], in_specs=[VMEM] * 2)(hardness, thickness)
     parts = call(
         scatter_kernel,
-        [(16, 8, 128)] * N_LAYER,
+        [(N_CHIP, 16, 8, 128)] * 2,
         scratch=[
             pltpu.VMEM((3 * PIECES * 96, DEPTH), jnp.bfloat16),
             pltpu.VMEM((256, DEPTH), jnp.bfloat16),
@@ -438,11 +449,11 @@
         flops=3600000000,
         limit=16,
     )(me, arrived, stiff)
-    parts = to_layers(parts)
+    parts = to_layers(*parts)
     (blocks,) = call(
         prepare_kernel, [(7, WB, 8, 128)], scratch=[pltpu.VMEM((6, WIDE, 128), F32)], in_specs=[VMEM]
     )(arrived)
-    (chunks,) = call(chunks_kernel, [(N_TILE, 4, 8, 128)], in_specs=[VMEM] * N_LAYER)(*parts)
+    (chunks,) = call(chunks_kernel, [(N_TILE, 4, 8, 128)], in_specs=[VMEM] * N_CHIP)(*parts)
     chunks = exchange(chunks, "tile")
     (shares,) = call(
         solve_kernel,

time: 86.1 us -> 83.8 us (0.973)
  starting transfers between devices: 23.3 us -> 19.5 us
  blocking collectives: 18.1 us -> 19.6 us
    ppermute x7 -> x4, starting transfers between devices: 11.1 us -> 7.27 us  [the longest x3 4.88 us: to_layers(): lax.ppermute(blocks[d], 'layer', [(i, (i + 2 * d) % N_LAYER) for i in ran...]
    all_to_all x1, blocking collectives: 18.1 us -> 19.6 us  [exchange(): return lax.all_to_all(x, axis, split_axis=0, concat_axis=0, tiled=True)]
    ppermute x7 -> x4, waiting for transfers between devices: 2.86 us -> 3.42 us  [the longest x3 2.26 us: to_layers(): lax.ppermute(blocks[d], 'layer', [(i, (i + 2 * d) % N_LAYER) for i in ran...]
    pallas_call x2 -> x3, Pallas kernels: 6.48 us -> 6.57 us  [the longest x1 5.28 us: on_device(): call(scatter_kernel, [(N_CHIP, 16, 8, 128)] * 2, scratch=[pltpu.VMEM((3 *...]
  transfers between devices with their start and end apart: 9 -> 6, of which waited for: 6 -> 5; matrix products, arithmetic and copies ran while one was open for 0% -> 0% of each run, Pallas kernels for 1% -> 1%
where the time goes in v5:
time: 83.8 us; the launch traced here: 83.4 us
  waiting for transfers between devices  22.4 us (27%)
  Pallas kernels  21.2 us (25%)
  blocking collectives  19.6 us (23%)
  starting transfers between devices  19.5 us (23%)
    all_to_all x1, blocking collectives, exchange(): return lax.all_to_all(x, axis, split_axis=0, concat_axis=0, tiled=True)  19.6 us
    all_to_all x2, waiting for transfers between devices, exchange(): return lax.all_to_all(x, axis, split_axis=0, concat_axis=0, tiled=True)  19 us
    all_to_all x2, starting transfers between devices, exchange(): return lax.all_to_all(x, axis, split_axis=0, concat_axis=0, tiled=True)  12.3 us
    pallas_call x1, Pallas kernels, on_device(): call(solve_kernel, [(N_TILE * N_LAYER * 5, 128)], scratch=[pltpu.VMEM((3,...  9.66 us
    pallas_call x1, Pallas kernels, on_device(): call(scatter_kernel, [(N_CHIP, 16, 8, 128)] * 2, scratch=[pltpu.VMEM((3 *...  5.28 us
    ppermute x3, starting transfers between devices, to_layers(): lax.ppermute(blocks[d], 'layer', [(i, (i + 2 * d) % N_LAYER) for i in ran...  4.88 us
    pallas_call x1, Pallas kernels, on_device(): call(pack_kernel, [(N_TILE * PACK_ROWS, 128)], in_specs=[SMEM] * 2 + [VME...  3.11 us
    ppermute x1, starting transfers between devices, to_layers(): moved = lax.ppermute(other, 'layer', [(i, i ^ 1) for i in range(N_LAYER)])  2.39 us
  transfers between devices with their start and end apart: 6, of which 5 were waited for; matrix products, arithmetic and copies ran while one was open for 0% of the time, Pallas kernels for 1%

profile of v5, /device:TPU:1, one launch (start us, length us, event | category | flops | bytes accessed | tf_op | source)
XLA Modules:
  0.0 83.4 jit_solution(2497551267312146097)
XLA Ops:
  0.6 3.1 %shard_map.131 = f32[1408,128]{1,0:T(8,128)} custom-call(s32[1]{0:T(128)} %bitcast.me_ref, s32[1,16]{1,0:T(1,128)} %bitcast.19, s32[16,512]{1,0:T(8,128)} %bitcast.15, f32[16,512]{1,0:T(8,128)} %bitcast.16, f32[16,512]{1,0:T(8,128)} %bitcast.17, f32[16,512]{1,0:T(8,128)} %bitcast.18, f32[2,8,3072]{2,1,0:T(8,128)} %guess_ref.1, f32[8,3072]{1,0:T(8,128)} %fric_ref.1, ...), custom_call_target="tpu_custom_call" | custom-call | flops 1000000 | bytes 1000000 | tf_op jit(solution)/shard_map/pallas_call | solution.py:432
  3.7 0.0 copy-start
  3.7 0.0 copy-start.1
  3.8 8.7 %all-to-all-start = ((f32[16,88,128]{2,1,0:T(8,128)}), f32[16,88,128]{2,1,0:T(8,128)S(1)}, u32[]{:S(2)}, u32[]{:S(2)}) async-start(f32[16,88,128]{2,1,0:T(8,128)} %bitcast.14), calls=%async_computation | async-start | bytes 1441792 | tf_op jit(solution)/shard_map/all_to_all | solution.py:413
  12.5 0.0 copy-done
  12.5 0.0 copy-done.1
  12.5 12.1 %all-to-all-done = f32[16,88,128]{2,1,0:T(8,128)S(1)} async-done(((f32[16,88,128]{2,1,0:T(8,128)}), f32[16,88,128]{2,1,0:T(8,128)S(1)}, u32[]{:S(2)}, u32[]{:S(2)}) %all-to-all-start) | async-done | bytes 720928 | tf_op jit(solution)/shard_map/all_to_all | solution.py:413
  24.7 5.3 %shard_map.133 = (f32[4,16,8,128]{3,2,1,0:T(8,128)S(1)}, f32[4,16,8,128]{3,2,1,0:T(8,128)S(1)}) custom-call(s32[1]{0:T(128)} %bitcast.me_ref, f32[1408,128]{1,0:T(8,128)S(1)} %bitcast.10, f32[8,3072]{1,0:T(8,128)S(1)} %shard_map.132.stiff_ref), custom_call_target="tpu_custom_call" | custom-call | flops 3600000000 | bytes 1000000 | tf_op jit(solution)/shard_map/pallas_call | solution.py:439
  29.9 2.4 %collective-permute-start = (f32[4,16,8,128]{3,2,1,0:T(8,128)S(1)}, f32[4,16,8,128]{3,2,1,0:T(8,128)S(1)}, u32[]{:S(2)}, u32[]{:S(2)}) collective-permute-start(f32[4,16,8,128]{3,2,1,0:T(8,128)S(1)} %get-tuple-element.9), channel_id=1, source_target_pairs={{0,1},{1,0},{2,3},{3,2},{4,5},{5,4},{6,7},{7,6},{8,9},{9,8},{10,11... | collective-permute-start | bytes 786440 | tf_op jit(solution)/shard_map/ppermute | solution.py:417
  32.3 1.2 %collective-permute-done.b_ref = f32[4,16,8,128]{3,2,1,0:T(8,128)S(1)} collective-permute-done((f32[4,16,8,128]{3,2,1,0:T(8,128)S(1)}, f32[4,16,8,128]{3,2,1,0:T(8,128)S(1)}, u32[]{:S(2)}, u32[]{:S(2)}) %collective-permute-start) | collective-permute-done | bytes 262176 | tf_op jit(solution)/shard_map/ppermute | solution.py:417
  33.5 1.3 %collective-permute-start.1 = (f32[16,8,128]{2,1,0:T(8,128)S(1)}, f32[16,8,128]{2,1,0:T(8,128)S(1)}, u32[]{:S(2)}, u32[]{:S(2)}) collective-permute-start(f32[16,8,128]{2,1,0:T(8,128)S(1)} %get-tuple-element.11), channel_id=1, source_target_pairs={{0,2},{1,3},{2,4},{3,5},{4,6},{5,7},{6,0},{7,1},{8,10},{9,11},{10,... | collective-permute-start | bytes 196616 | tf_op jit(solution)/shard_map/ppermute | solution.py:422
  34.8 2.5 %collective-permute-start.2 = (f32[16,8,128]{2,1,0:T(8,128)S(1)}, f32[16,8,128]{2,1,0:T(8,128)S(1)}, u32[]{:S(2)}, u32[]{:S(2)}) collective-permute-start(f32[16,8,128]{2,1,0:T(8,128)S(1)} %get-tuple-element.12), channel_id=1, source_target_pairs={{0,4},{1,5},{2,6},{3,7},{4,0},{5,1},{6,2},{7,3},{8,12},{9,13},{10,... | collective-permute-start | bytes 196616 | tf_op jit(solution)/shard_map/ppermute | solution.py:422
  37.3 1.2 %collective-permute-start.3 = (f32[16,8,128]{2,1,0:T(8,128)S(1)}, f32[16,8,128]{2,1,0:T(8,128)S(1)}, u32[]{:S(2)}, u32[]{:S(2)}) collective-permute-start(f32[16,8,128]{2,1,0:T(8,128)S(1)} %get-tuple-element.13), channel_id=1, source_target_pairs={{0,6},{1,7},{2,0},{3,1},{4,2},{5,3},{6,4},{7,5},{8,14},{9,15},{10,... | collective-permute-start | bytes 196616 | tf_op jit(solution)/shard_map/ppermute | solution.py:422
  38.4 0.0 collective-permute-done.1.refs_1_
  38.4 1.8 %collective-permute-done.2.refs_2_ = f32[16,8,128]{2,1,0:T(8,128)S(1)} collective-permute-done((f32[16,8,128]{2,1,0:T(8,128)S(1)}, f32[16,8,128]{2,1,0:T(8,128)S(1)}, u32[]{:S(2)}, u32[]{:S(2)}) %collective-permute-start.2) | collective-permute-done | bytes 65568 | tf_op jit(solution)/shard_map/ppermute | solution.py:422
  40.2 0.5 collective-permute-done.3.refs_3_
  40.7 1.3 %shard_map.135 = f32[16,4,8,128]{3,2,1,0:T(8,128)} custom-call(f32[16,8,128]{2,1,0:T(8,128)S(1)} %get-tuple-element.10.refs_0_, f32[16,8,128]{2,1,0:T(8,128)S(1)} %collective-permute-done.1.refs_1_, f32[16,8,128]{2,1,0:T(8,128)S(1)} %collective-permute-done.2.refs_2_, f32[16,8,128]{2,1,0:T(8,128)S(1)} %collective-permute-done.3.refs_3_), custom_call_target="tpu_custom_call" | custom-call | flops 1000000 | bytes 1000000 | tf_op jit(solution)/shard_map/pallas_call | solution.py:456
  41.9 3.5 %all-to-all-start.1 = ((f32[16,4,8,128]{3,2,1,0:T(8,128)}), f32[16,4,8,128]{3,2,1,0:T(8,128)S(1)}, u32[]{:S(2)}, u32[]{:S(2)}) async-start(f32[16,4,8,128]{3,2,1,0:T(8,128)} %shard_map.135), calls=%async_computation.1 | async-start | bytes 524288 | tf_op jit(solution)/shard_map/all_to_all | solution.py:413
  45.5 0.4 shard_map.136.blk
  45.9 6.9 %all-to-all-done.1.z_ref = f32[16,4,8,128]{3,2,1,0:T(8,128)S(1)} async-done(((f32[16,4,8,128]{3,2,1,0:T(8,128)}), f32[16,4,8,128]{3,2,1,0:T(8,128)S(1)}, u32[]{:S(2)}, u32[]{:S(2)}) %all-to-all-start.1) | async-done | bytes 262176 | tf_op jit(solution)/shard_map/all_to_all | solution.py:413
  52.8 9.7 %shard_map.137 = f32[640,128]{1,0:T(8,128)S(1)} custom-call(f32[16,4,8,128]{3,2,1,0:T(8,128)S(1)} %all-to-all-done.1.z_ref, f32[7,23,8,128]{3,2,1,0:T(8,128)S(1)} %shard_map.136.blk), custom_call_target="tpu_custom_call" | custom-call | flops 3600000000 | bytes 1000000 | tf_op jit(solution)/shard_map/pallas_call | solution.py:458
  62.4 19.6 %all_to_all.19 = f32[128,640,1]{1,2,0:T(1,128)S(1)} all-to-all(f32[128,640,1]{1,2,0:T(1,128)S(1)} %bitcast.13), channel_id=1, replica_groups=mesh['tile'=16,'layer'=8] {'tile','layer'}, dimensions={0} | all-to-all | bytes 655360 | tf_op jit(solution)/shard_map/all_to_all | solution.py:413
  82.0 1.4 %shard_map.138 = (f32[2,8,3072]{2,1,0:T(8,128)}, f32[8,3072]{1,0:T(8,128)}) custom-call(f32[640,128]{1,0:T(8,128)S(1)} %bitcast.12), custom_call_target="tpu_custom_call" | custom-call | flops 1000000 | bytes 1000000 | tf_op jit(solution)/shard_map/pallas_call | solution.py:480
  (2 shorter events, 0.1 us)
Async XLA Ops:
  3.7 8.7 %copy-start = (f32[4,8,3072]{2,1,0:T(8,128)S(1)}, f32[4,8,3072]{2,1,0:T(8,128)}, u32[]{:S(2)}) copy-start(f32[4,8,3072]{2,1,0:T(8,128)} %hard_ref.1) | copy-start | bytes 1179652
  3.7 8.8 %copy-start.1 = (f32[8,3072]{1,0:T(8,128)S(1)}, f32[8,3072]{1,0:T(8,128)}, u32[]{:S(2)}) copy-start(f32[8,3072]{1,0:T(8,128)} %thick_ref.1) | copy-start | bytes 294916
  3.8 20.9 %all-to-all-start = ((f32[16,88,128]{2,1,0:T(8,128)}), f32[16,88,128]{2,1,0:T(8,128)S(1)}, u32[]{:S(2)}, u32[]{:S(2)}) async-start(f32[16,88,128]{2,1,0:T(8,128)} %bitcast.14), calls=%async_computation | async-start | bytes 1441792 | tf_op jit(solution)/shard_map/all_to_all | solution.py:413
  29.9 3.6 %collective-permute-start = (f32[4,16,8,128]{3,2,1,0:T(8,128)S(1)}, f32[4,16,8,128]{3,2,1,0:T(8,128)S(1)}, u32[]{:S(2)}, u32[]{:S(2)}) collective-permute-start(f32[4,16,8,128]{3,2,1,0:T(8,128)S(1)} %get-tuple-element.9), channel_id=1, source_target_pairs={{0,1},{1,0},{2,3},{3,2},{4,5},{5,4},{6,7},{7,6},{8,9},{9,8},{10,11... | collective-permute-start | bytes 786440 | tf_op jit(solution)/shard_map/ppermute | solution.py:417
  33.5 4.9 %collective-permute-start.1 = (f32[16,8,128]{2,1,0:T(8,128)S(1)}, f32[16,8,128]{2,1,0:T(8,128)S(1)}, u32[]{:S(2)}, u32[]{:S(2)}) collective-permute-start(f32[16,8,128]{2,1,0:T(8,128)S(1)} %get-tuple-element.11), channel_id=1, source_target_pairs={{0,2},{1,3},{2,4},{3,5},{4,6},{5,7},{6,0},{7,1},{8,10},{9,11},{10,... | collective-permute-start | bytes 196616 | tf_op jit(solution)/shard_map/ppermute | solution.py:422
  34.8 5.4 %collective-permute-start.2 = (f32[16,8,128]{2,1,0:T(8,128)S(1)}, f32[16,8,128]{2,1,0:T(8,128)S(1)}, u32[]{:S(2)}, u32[]{:S(2)}) collective-permute-start(f32[16,8,128]{2,1,0:T(8,128)S(1)} %get-tuple-element.12), channel_id=1, source_target_pairs={{0,4},{1,5},{2,6},{3,7},{4,0},{5,1},{6,2},{7,3},{8,12},{9,13},{10,... | collective-permute-start | bytes 196616 | tf_op jit(solution)/shard_map/ppermute | solution.py:422
  37.3 3.4 %collective-permute-start.3 = (f32[16,8,128]{2,1,0:T(8,128)S(1)}, f32[16,8,128]{2,1,0:T(8,128)S(1)}, u32[]{:S(2)}, u32[]{:S(2)}) collective-permute-start(f32[16,8,128]{2,1,0:T(8,128)S(1)} %get-tuple-element.13), channel_id=1, source_target_pairs={{0,6},{1,7},{2,0},{3,1},{4,2},{5,3},{6,4},{7,5},{8,14},{9,15},{10,... | collective-permute-start | bytes 196616 | tf_op jit(solution)/shard_map/ppermute | solution.py:422
  41.9 10.8 %all-to-all-start.1 = ((f32[16,4,8,128]{3,2,1,0:T(8,128)}), f32[16,4,8,128]{3,2,1,0:T(8,128)S(1)}, u32[]{:S(2)}, u32[]{:S(2)}) async-start(f32[16,4,8,128]{3,2,1,0:T(8,128)} %shard_map.135), calls=%async_computation.1 | async-start | bytes 524288 | tf_op jit(solution)/shard_map/all_to_all | solution.py:413

commit v6 on v5

--- a/solution.py
+++ b/solution.py
@@ -26,7 +26,7 @@
 PACK_ROWS = 8 * 11
 PIECES = 3
 UNROLL = 20
-DEPTH = 2048
+DEPTH = 4096
 OBS_ROWS = PACK_ROWS
 OBS_AT = 72
 
@@ -447,12 +447,13 @@
         ],
         in_specs=[SMEM] + [VMEM] * 2,
         flops=3600000000,
-        limit=16,
+        limit=24,
     )(me, arrived, stiff)
     parts = to_layers(*parts)
     (blocks,) = call(
         prepare_kernel, [(7, WB, 8, 128)], scratch=[pltpu.VMEM((6, WIDE, 128), F32)], in_specs=[VMEM]
     )(arrived)
+    blocks, parts[0] = lax.optimization_barrier((blocks, parts[0]))
     (chunks,) = call(chunks_kernel, [(N_TILE, 4, 8, 128)], in_specs=[VMEM] * N_CHIP)(*parts)
     chunks = exchange(chunks, "tile")
     (shares,) = call(

time: 83.8 us -> 82.6 us (0.986)
  blocking collectives: 19.6 us -> 30.2 us
  waiting for transfers between devices: 22.4 us -> 15.1 us
  starting transfers between devices: 19.5 us -> 16 us
  Pallas kernels: 21.2 us -> 20.3 us
    all_to_all x1 -> x2, blocking collectives: 19.6 us -> 30.2 us  [exchange(): return lax.all_to_all(x, axis, split_axis=0, concat_axis=0, tiled=True)]
    all_to_all x2 -> x1, waiting for transfers between devices: 19 us -> 12.1 us  [exchange(): return lax.all_to_all(x, axis, split_axis=0, concat_axis=0, tiled=True)]
    all_to_all x2 -> x1, starting transfers between devices: 12.3 us -> 8.73 us  [exchange(): return lax.all_to_all(x, axis, split_axis=0, concat_axis=0, tiled=True)]
  transfers between devices with their start and end apart: 6 -> 5, of which waited for: 5 -> 4; matrix products, arithmetic and copies ran while one was open for 0% -> 0% of each run, Pallas kernels for 1% -> 1%
where the time goes in v6:
time: 82.6 us; the launch traced here: 82.3 us
  blocking collectives  30.2 us (37%)
  Pallas kernels  20.3 us (25%)
  starting transfers between devices  16 us (19%)
  waiting for transfers between devices  15.1 us (18%)
    all_to_all x2, blocking collectives, exchange(): return lax.all_to_all(x, axis, split_axis=0, concat_axis=0, tiled=True)  30.2 us
    all_to_all x1, waiting for transfers between devices, exchange(): return lax.all_to_all(x, axis, split_axis=0, concat_axis=0, tiled=True)  12.1 us
    pallas_call x1, Pallas kernels, on_device(): call(solve_kernel, [(N_TILE * N_LAYER * 5, 128)], scratch=[pltpu.VMEM((3,...  9.66 us
    all_to_all x1, starting transfers between devices, exchange(): return lax.all_to_all(x, axis, split_axis=0, concat_axis=0, tiled=True)  8.73 us
    pallas_call x1, Pallas kernels, on_device(): call(scatter_kernel, [(N_CHIP, 16, 8, 128)] * 2, scratch=[pltpu.VMEM((3 *...  5.07 us
    ppermute x3, starting transfers between devices, to_layers(): lax.ppermute(blocks[d], 'layer', [(i, (i + 2 * d) % N_LAYER) for i in ran...  4.88 us
    pallas_call x1, Pallas kernels, on_device(): call(pack_kernel, [(N_TILE * PACK_ROWS, 128)], in_specs=[SMEM] * 2 + [VME...  3.12 us
    ppermute x1, starting transfers between devices, to_layers(): moved = lax.ppermute(other, 'layer', [(i, i ^ 1) for i in range(N_LAYER)])  2.39 us
  transfers between devices with their start and end apart: 5, of which 4 were waited for; matrix products, arithmetic and copies ran while one was open for 0% of the time, Pallas kernels for 1%

profile of v6, /device:TPU:1, one launch (start us, length us, event | category | flops | bytes accessed | tf_op | source)
XLA Modules:
  0.0 82.3 jit_solution(9083840519548968499)
XLA Ops:
  0.6 3.1 %shard_map.131 = f32[1408,128]{1,0:T(8,128)} custom-call(s32[1]{0:T(128)} %bitcast.me_ref, s32[1,16]{1,0:T(1,128)} %bitcast.19, s32[16,512]{1,0:T(8,128)} %bitcast.15, f32[16,512]{1,0:T(8,128)} %bitcast.16, f32[16,512]{1,0:T(8,128)} %bitcast.17, f32[16,512]{1,0:T(8,128)} %bitcast.18, f32[2,8,3072]{2,1,0:T(8,128)} %guess_ref.1, f32[8,3072]{1,0:T(8,128)} %fric_ref.1, ...), custom_call_target="tpu_custom_call" | custom-call | flops 1000000 | bytes 1000000 | tf_op jit(solution)/shard_map/pallas_call | solution.py:432
  3.8 0.0 copy-start
  3.8 0.0 copy-start.1
  3.8 8.7 %all-to-all-start = ((f32[16,88,128]{2,1,0:T(8,128)}), f32[16,88,128]{2,1,0:T(8,128)S(1)}, u32[]{:S(2)}, u32[]{:S(2)}) async-start(f32[16,88,128]{2,1,0:T(8,128)} %bitcast.14), calls=%async_computation | async-start | bytes 1441792 | tf_op jit(solution)/shard_map/all_to_all | solution.py:413
  12.5 0.0 copy-done
  12.5 0.0 copy-done.1
  12.6 12.1 %all-to-all-done = f32[16,88,128]{2,1,0:T(8,128)S(1)} async-done(((f32[16,88,128]{2,1,0:T(8,128)}), f32[16,88,128]{2,1,0:T(8,128)S(1)}, u32[]{:S(2)}, u32[]{:S(2)}) %all-to-all-start) | async-done | bytes 720928 | tf_op jit(solution)/shard_map/all_to_all | solution.py:413
  24.7 5.1 %shard_map.134 = (f32[4,16,8,128]{3,2,1,0:T(8,128)S(1)}, f32[4,16,8,128]{3,2,1,0:T(8,128)S(1)}) custom-call(s32[1]{0:T(128)} %bitcast.me_ref, f32[1408,128]{1,0:T(8,128)S(1)} %bitcast.10, f32[8,3072]{1,0:T(8,128)S(1)} %shard_map.133.stiff_ref), custom_call_target="tpu_custom_call" | custom-call | flops 3600000000 | bytes 1000000 | tf_op jit(solution)/shard_map/pallas_call | solution.py:439
  29.8 2.4 %collective-permute-start = (f32[4,16,8,128]{3,2,1,0:T(8,128)S(1)}, f32[4,16,8,128]{3,2,1,0:T(8,128)S(1)}, u32[]{:S(2)}, u32[]{:S(2)}) collective-permute-start(f32[4,16,8,128]{3,2,1,0:T(8,128)S(1)} %get-tuple-element.11), channel_id=1, source_target_pairs={{0,1},{1,0},{2,3},{3,2},{4,5},{5,4},{6,7},{7,6},{8,9},{9,8},{10,11... | collective-permute-start | bytes 786440 | tf_op jit(solution)/shard_map/ppermute | solution.py:417
  32.1 1.2 %collective-permute-done.b_ref = f32[4,16,8,128]{3,2,1,0:T(8,128)S(1)} collective-permute-done((f32[4,16,8,128]{3,2,1,0:T(8,128)S(1)}, f32[4,16,8,128]{3,2,1,0:T(8,128)S(1)}, u32[]{:S(2)}, u32[]{:S(2)}) %collective-permute-start) | collective-permute-done | bytes 262176 | tf_op jit(solution)/shard_map/ppermute | solution.py:417
  33.3 1.3 %collective-permute-start.1 = (f32[16,8,128]{2,1,0:T(8,128)S(1)}, f32[16,8,128]{2,1,0:T(8,128)S(1)}, u32[]{:S(2)}, u32[]{:S(2)}) collective-permute-start(f32[16,8,128]{2,1,0:T(8,128)S(1)} %get-tuple-element.14), channel_id=1, source_target_pairs={{0,2},{1,3},{2,4},{3,5},{4,6},{5,7},{6,0},{7,1},{8,10},{9,11},{10,... | collective-permute-start | bytes 196616 | tf_op jit(solution)/shard_map/ppermute | solution.py:422
  34.6 2.5 %collective-permute-start.2 = (f32[16,8,128]{2,1,0:T(8,128)S(1)}, f32[16,8,128]{2,1,0:T(8,128)S(1)}, u32[]{:S(2)}, u32[]{:S(2)}) collective-permute-start(f32[16,8,128]{2,1,0:T(8,128)S(1)} %get-tuple-element.15), channel_id=1, source_target_pairs={{0,4},{1,5},{2,6},{3,7},{4,0},{5,1},{6,2},{7,3},{8,12},{9,13},{10,... | collective-permute-start | bytes 196616 | tf_op jit(solution)/shard_map/ppermute | solution.py:422
  37.1 1.2 %collective-permute-start.3 = (f32[16,8,128]{2,1,0:T(8,128)S(1)}, f32[16,8,128]{2,1,0:T(8,128)S(1)}, u32[]{:S(2)}, u32[]{:S(2)}) collective-permute-start(f32[16,8,128]{2,1,0:T(8,128)S(1)} %get-tuple-element.16), channel_id=1, source_target_pairs={{0,6},{1,7},{2,0},{3,1},{4,2},{5,3},{6,4},{7,5},{8,14},{9,15},{10,... | collective-permute-start | bytes 196616 | tf_op jit(solution)/shard_map/ppermute | solution.py:422
  38.2 0.4 shard_map.132.blk
  38.6 0.0 collective-permute-done.1.refs_1_
  38.6 1.4 %collective-permute-done.2.refs_2_ = f32[16,8,128]{2,1,0:T(8,128)S(1)} collective-permute-done((f32[16,8,128]{2,1,0:T(8,128)S(1)}, f32[16,8,128]{2,1,0:T(8,128)S(1)}, u32[]{:S(2)}, u32[]{:S(2)}) %collective-permute-start.2) | collective-permute-done | bytes 65568 | tf_op jit(solution)/shard_map/ppermute | solution.py:422
  40.0 0.5 collective-permute-done.3.refs_3_
  40.5 0.6 shard_map.136
  41.0 10.3 %all_to_all.19.z_ref = f32[16,4,8,128]{3,2,1,0:T(8,128)S(1)} all-to-all(f32[16,4,8,128]{3,2,1,0:T(8,128)S(1)} %shard_map.136), channel_id=1, replica_groups=mesh['tile'=16,'layer'=8] {'tile'}, dimensions={0} | all-to-all | bytes 524288 | tf_op jit(solution)/shard_map/all_to_all | solution.py:413
  51.4 9.7 %shard_map.137 = f32[640,128]{1,0:T(8,128)S(1)} custom-call(f32[16,4,8,128]{3,2,1,0:T(8,128)S(1)} %all_to_all.19.z_ref, f32[7,23,8,128]{3,2,1,0:T(8,128)S(1)} %shard_map.132.blk), custom_call_target="tpu_custom_call" | custom-call | flops 3600000000 | bytes 1000000 | tf_op jit(solution)/shard_map/pallas_call | solution.py:459
  61.0 19.8 %all_to_all.20 = f32[128,640,1]{1,2,0:T(1,128)S(1)} all-to-all(f32[128,640,1]{1,2,0:T(1,128)S(1)} %bitcast.13), channel_id=1, replica_groups=mesh['tile'=16,'layer'=8] {'tile','layer'}, dimensions={0} | all-to-all | bytes 655360 | tf_op jit(solution)/shard_map/all_to_all | solution.py:413
  80.9 1.4 %shard_map.138 = (f32[2,8,3072]{2,1,0:T(8,128)}, f32[8,3072]{1,0:T(8,128)}) custom-call(f32[640,128]{1,0:T(8,128)S(1)} %bitcast.12), custom_call_target="tpu_custom_call" | custom-call | flops 1000000 | bytes 1000000 | tf_op jit(solution)/shard_map/pallas_call | solution.py:481
  (2 shorter events, 0.1 us)
Async XLA Ops:
  3.8 8.7 %copy-start = (f32[4,8,3072]{2,1,0:T(8,128)S(1)}, f32[4,8,3072]{2,1,0:T(8,128)}, u32[]{:S(2)}) copy-start(f32[4,8,3072]{2,1,0:T(8,128)} %hard_ref.1) | copy-start | bytes 1179652
  3.8 8.8 %copy-start.1 = (f32[8,3072]{1,0:T(8,128)S(1)}, f32[8,3072]{1,0:T(8,128)}, u32[]{:S(2)}) copy-start(f32[8,3072]{1,0:T(8,128)} %thick_ref.1) | copy-start | bytes 294916
  3.8 20.9 %all-to-all-start = ((f32[16,88,128]{2,1,0:T(8,128)}), f32[16,88,128]{2,1,0:T(8,128)S(1)}, u32[]{:S(2)}, u32[]{:S(2)}) async-start(f32[16,88,128]{2,1,0:T(8,128)} %bitcast.14), calls=%async_computation | async-start | bytes 1441792 | tf_op jit(solution)/shard_map/all_to_all | solution.py:413
  29.8 3.5 %collective-permute-start = (f32[4,16,8,128]{3,2,1,0:T(8,128)S(1)}, f32[4,16,8,128]{3,2,1,0:T(8,128)S(1)}, u32[]{:S(2)}, u32[]{:S(2)}) collective-permute-start(f32[4,16,8,128]{3,2,1,0:T(8,128)S(1)} %get-tuple-element.11), channel_id=1, source_target_pairs={{0,1},{1,0},{2,3},{3,2},{4,5},{5,4},{6,7},{7,6},{8,9},{9,8},{10,11... | collective-permute-start | bytes 786440 | tf_op jit(solution)/shard_map/ppermute | solution.py:417
  33.3 5.3 %collective-permute-start.1 = (f32[16,8,128]{2,1,0:T(8,128)S(1)}, f32[16,8,128]{2,1,0:T(8,128)S(1)}, u32[]{:S(2)}, u32[]{:S(2)}) collective-permute-start(f32[16,8,128]{2,1,0:T(8,128)S(1)} %get-tuple-element.14), channel_id=1, source_target_pairs={{0,2},{1,3},{2,4},{3,5},{4,6},{5,7},{6,0},{7,1},{8,10},{9,11},{10,... | collective-permute-start | bytes 196616 | tf_op jit(solution)/shard_map/ppermute | solution.py:422
  34.6 5.4 %collective-permute-start.2 = (f32[16,8,128]{2,1,0:T(8,128)S(1)}, f32[16,8,128]{2,1,0:T(8,128)S(1)}, u32[]{:S(2)}, u32[]{:S(2)}) collective-permute-start(f32[16,8,128]{2,1,0:T(8,128)S(1)} %get-tuple-element.15), channel_id=1, source_target_pairs={{0,4},{1,5},{2,6},{3,7},{4,0},{5,1},{6,2},{7,3},{8,12},{9,13},{10,... | collective-permute-start | bytes 196616 | tf_op jit(solution)/shard_map/ppermute | solution.py:422
  37.1 3.4 %collective-permute-start.3 = (f32[16,8,128]{2,1,0:T(8,128)S(1)}, f32[16,8,128]{2,1,0:T(8,128)S(1)}, u32[]{:S(2)}, u32[]{:S(2)}) collective-permute-start(f32[16,8,128]{2,1,0:T(8,128)S(1)} %get-tuple-element.16), channel_id=1, source_target_pairs={{0,6},{1,7},{2,0},{3,1},{4,2},{5,3},{6,4},{7,5},{8,14},{9,15},{10,... | collective-permute-start | bytes 196616 | tf_op jit(solution)/shard_map/ppermute | solution.py:422
